TPU v7x, 512 devices: a whole 4x4x16 slice. The times are simulated.
512 devices in a mesh: vocab: 64 (over x, z), batch: 8 (over y, core).
Axes of the slice: x: 4, y: 4, z: 16, core: 2. Of those that a mesh axis runs over, the one named last changes fastest.
Arguments:
- hidden: bfloat16 [1024, 4096], P('batch', 'vocab'), may hold values from -6 to 6
- head_weight: bfloat16 [4096, 65536], P('batch', 'vocab'), may hold values from -0.09375 to 0.09375
- passages: bfloat16 [2048, 65536], P('batch', 'vocab'), may hold values from -6 to 6
- pair_query: int32 [3072], P('batch'), may hold values from 0 to 63
- pair_passage: int32 [3072], P('batch'), may hold values from 0 to 255
- pair_count: int32 [8], P('batch'), may hold values from 128 to 384, as said below
- teacher: float32 [3072], P('batch'), may hold values from -24 to 24
Outputs:
- pooled: bfloat16 [64, 65536], P('batch', 'vocab')
- grad_hidden: bfloat16 [1024, 4096], P('batch', 'vocab')
- loss_value: float32 [], replicated
Inputs may be any that keep to these rules, and one draw needn't show every extreme that they name: `pair_count`: slots of a group at or past its count are padding; some group has all 384 slots live.
All inputs are finite; a program needn't handle non-finite values.
Results may differ from a plain program's by a relative error of at most 0.012.
Values may be sent and summed in bfloat16 or wider, within the bound.
No kernel may reach another device: no remote copies, remote signals or barrier semaphores. Data moves between devices by JAX's collectives and lax.ppermute only.
A program may use at most 64 MiB of HBM per device.

v0:
```python
import functools
import math

import jax
import jax.numpy as jnp
from jax import lax
from jax.experimental import pallas as pl
from jax.experimental.pallas import tpu as pltpu
from jax.sharding import Mesh
from jax.sharding import PartitionSpec as P


VOCAB = 65536
QLEN = 16
LANES = 128
F32 = jnp.float32
BF16 = jnp.bfloat16


def ring(n, step):
    return [(i, (i + step) % n) for i in range(n)]


def spread(value, axes, n):
    return lax.all_to_all(jnp.broadcast_to(value[None], (n,) + value.shape), axes, 0, 0, tiled=True)


def dot(a, b, ca, cb):
    return lax.dot_general(a, b, (((ca,), (cb,)), ((), ())), preferred_element_type=F32)


ANY = pl.BlockSpec(memory_space=pl.ANY)
SMEM = pl.BlockSpec(memory_space=pltpu.SMEM)
WHOLE = pl.BlockSpec(memory_space=pltpu.VMEM)


def forward_kernel(nb, place, mine, theirs, *refs):
    blocks, (pooled, slope, feats, held, total, sems) = refs[:nb], refs[nb:]
    rows = held.shape[1]
    tok = mine.shape[1]
    copies = [
        pltpu.make_async_copy(mine, feats.at[:, pl.ds(0, tok)], sems.at[nb]),
        pltpu.make_async_copy(theirs, feats.at[:, pl.ds(tok, tok)], sems.at[nb + 1]),
    ]
    copies += [pltpu.make_async_copy(blocks[k], held.at[k], sems.at[k]) for k in range(nb)]
    for copy in copies:
        copy.start()
    copies[0].wait()
    copies[1].wait()
    for k in range(nb):
        copies[2 + k].wait()
        start = pl.multiple_of(place[k], rows)
        term = dot(feats[pl.ds(start, rows), :], held[k], 0, 0)
        if k:
            total[...] += term
        else:
            total[...] = term
    logits = total[...]
    positive = jnp.maximum(logits, 0.0)
    slope[...] = jnp.where(logits > 0, 1.0 / (1.0 + positive), 0.0)
    sums = jnp.log1p(positive).reshape(-1, QLEN, logits.shape[1]).sum(1)
    half = sums.shape[0] // 2
    first, second = sums[:half], sums[half:]
    swapped = place[nb] == 1
    pooled[:half, :] = jnp.where(swapped, second, first).astype(BF16)
    pooled[half:, :] = jnp.where(swapped, first, second).astype(BF16)


def forward(place, mine, theirs, blocks):
    nb, (rows, cols) = len(blocks), blocks[0].shape
    depth, tok = mine.shape
    queries = 2 * tok // QLEN
    return pl.pallas_call(
        functools.partial(forward_kernel, nb),
        name="forward",
        out_shape=(
            jax.ShapeDtypeStruct((queries, cols), BF16),
            jax.ShapeDtypeStruct((2 * tok, cols), F32),
        ),
        in_specs=[SMEM] + [ANY] * (2 + nb),
        out_specs=(WHOLE, WHOLE),
        scratch_shapes=[
            pltpu.VMEM((depth, 2 * tok), BF16),
            pltpu.VMEM((nb, rows, cols), BF16),
            pltpu.VMEM((2 * tok, cols), F32),
            pltpu.SemaphoreType.DMA((nb + 2,)),
        ],
        cost_estimate=pl.CostEstimate(
            flops=4 * tok * depth * cols,
            bytes_accessed=2 * depth * (2 * tok + cols) + 8 * tok * cols,
            transcendentals=2 * tok * cols,
        ),
        compiler_params=pltpu.CompilerParams(vmem_limit_bytes=32 << 20),
    )(place, mine, theirs, *blocks)


def backward_kernel(nb, place, grad, slope, *refs):
    blocks, (out, held, sems) = refs[:nb], refs[nb:]
    rows = held.shape[1]
    copies = [pltpu.make_async_copy(blocks[k], held.at[k], sems.at[k]) for k in range(nb)]
    for copy in copies:
        copy.start()
    tok, cols = slope.shape
    spread_grad = jnp.broadcast_to(grad[...][:, None, :], (tok // QLEN, QLEN, cols))
    logit_grad = (spread_grad.reshape(tok, cols) * slope[...]).astype(BF16)
    for k in range(nb):
        copies[k].wait()
        start = pl.multiple_of(place[k], rows)
        out[pl.ds(start, rows), :] = dot(held[k], logit_grad, 1, 1).astype(BF16)


def backward(place, grad, slope, blocks):
    nb, (rows, cols) = len(blocks), blocks[0].shape
    tok = slope.shape[0]
    depth = nb * rows
    return pl.pallas_call(
        functools.partial(backward_kernel, nb),
        name="backward",
        out_shape=jax.ShapeDtypeStruct((depth, tok), BF16),
        in_specs=[SMEM, WHOLE, WHOLE] + [ANY] * nb,
        out_specs=WHOLE,
        scratch_shapes=[
            pltpu.VMEM((nb, rows, cols), BF16),
            pltpu.SemaphoreType.DMA((nb,)),
        ],
        cost_estimate=pl.CostEstimate(
            flops=2 * tok * depth * cols,
            bytes_accessed=2 * depth * (tok + cols) + 4 * tok * cols,
            transcendentals=0,
        ),
        compiler_params=pltpu.CompilerParams(vmem_limit_bytes=32 << 20),
    )(place, grad, slope, *blocks)


def step(hidden, head, passages, pair_query, pair_passage, pair_count, teacher):
    nx, nz = lax.axis_size("x"), lax.axis_size("z")
    ny, nc = lax.axis_size("y"), lax.axis_size("c")
    y, c = lax.axis_index("y"), lax.axis_index("c")
    tok, feat = hidden.shape
    rows, cols = head.shape
    half = cols // nc
    batch = ny * nc
    queries = tok // QLEN
    swap = ring(nc, 1)
    plus, minus = ring(ny, 1), ring(ny, ny - 1)

    own = lax.dynamic_slice_in_dim(head, c * half, half, 1)
    sent = lax.dynamic_slice_in_dim(head, (1 - c) * half, half, 1)
    prev_own = lax.ppermute(own, "y", plus)
    next_own = lax.ppermute(own, "y", minus)
    pair = lax.ppermute(sent, "c", swap)
    next_pair = lax.ppermute(pair, "y", minus)
    prev_pair = lax.ppermute(pair, "y", plus)
    far_own = lax.ppermute(prev_own, "y", plus)
    far_pair = lax.ppermute(next_pair, "y", minus)

    part = spread(hidden.T, "z", nz).reshape(nz * feat, tok)
    mine = spread(part, "x", nx).reshape(nx * nz * feat, tok)
    theirs = lax.ppermute(mine, "c", swap)

    held = [
        (0, 0, own),
        (0, 1, pair),
        (ny - 1, 0, prev_own),
        (1, 0, next_own),
        (ny - 1, 1, prev_pair),
        (1, 1, next_pair),
        (2, 0, far_own),
        (2, 1, far_pair),
    ]
    blocks = [block for _, _, block in held]
    steps = jnp.array([step for step, _, _ in held], jnp.int32)
    others = jnp.array([other for _, other, _ in held], jnp.int32)
    owner = ((y + steps) % ny) * nc + (c + others) % nc
    place = jnp.concatenate([owner * rows, c[None]]).astype(jnp.int32)

    both, slope = forward(place, mine, theirs, blocks)
    every = spread(both, ("y", "c"), batch).reshape(ny, nc, nc * queries, half)
    halves = [every[:, i].reshape(batch * queries, half) for i in range(nc)]
    wide = jnp.concatenate(halves, axis=1)
    pooled = lax.dynamic_slice_in_dim(wide, (y * nc + c) * queries, queries, 0)

    inv_root = 1.0 / math.sqrt(VOCAB)
    slots = pair_query.shape[0]
    n_query, n_passage = batch * queries, passages.shape[0]
    table = dot(passages, wide, 1, 1)
    query_hot = (pair_query[None, :] == jnp.arange(n_query, dtype=jnp.int32)[:, None]).astype(F32)
    passage_hot = (
        pair_passage[None, :] == jnp.arange(n_passage, dtype=jnp.int32)[:, None]
    ).astype(F32)
    spread_table = jnp.dot(table, query_hot, precision=lax.Precision.HIGHEST)
    partial_value = (spread_table * passage_hot).sum(0)
    packed = jnp.pad(partial_value, (0, -slots % 512)).reshape(-1, LANES)
    packed = spread(packed, ("x", "z"), nx * nz).sum(0)
    scores = packed.reshape(-1)[:slots] * inv_root

    is_live = jnp.arange(slots, dtype=jnp.int32) < pair_count[0]
    residual = jnp.where(is_live, scores - teacher, 0.0)
    error = jnp.sum(residual * residual)
    pair_grad = 2.0 * residual * inv_root
    pair_table = lax.dot_general(
        query_hot,
        passage_hot * pair_grad[None, :],
        (((1,), (1,)), ((), ())),
        precision=lax.Precision.HIGHEST,
    )
    table_high = pair_table.astype(BF16)
    table_low = (pair_table - table_high.astype(F32)).astype(BF16)
    query_terms = dot(table_high, passages, 1, 0) + dot(table_low, passages, 1, 0)
    terms = jnp.stack(
        [
            query_terms[:, i * half : (i + 1) * half].reshape(ny, nc * queries, half)
            for i in range(nc)
        ],
        axis=1,
    ).reshape(batch, nc * queries, half)
    terms = jnp.concatenate(
        [terms, jnp.broadcast_to(error, (batch, nc * queries, LANES))], axis=2
    )
    terms = lax.all_to_all(terms, ("y", "c"), 0, 0, tiled=True).sum(0)
    loss_value = terms[0, half] / (slots * batch)
    grads = terms[:, :half].reshape(nc, queries, half)
    grad_mine = lax.dynamic_index_in_dim(grads, c, 0, keepdims=False)
    grad_theirs = lax.dynamic_index_in_dim(grads, 1 - c, 0, keepdims=False)

    terms_theirs = backward(place, grad_theirs, slope[tok:], blocks)
    terms_pair = lax.ppermute(terms_theirs, "c", swap)
    terms_mine = backward(place, grad_mine, slope[:tok], blocks)
    hidden_terms = (terms_mine.astype(F32) + terms_pair.astype(F32)).astype(BF16)
    hidden_terms = hidden_terms.reshape(nx, nz * feat, tok)
    over_x = lax.all_to_all(hidden_terms, "x", 0, 0, tiled=True)
    over_x = over_x.astype(F32).sum(0).astype(BF16).reshape(nz, feat, tok)
    over_z = lax.all_to_all(over_x, "z", 0, 0, tiled=True)
    grad_hidden = over_z.astype(F32).sum(0).astype(BF16).T
    return (pooled, grad_hidden, loss_value)


def solution(mesh, sizes=(4, 16, 4, 2)):
    mesh = Mesh(mesh.devices.reshape(sizes), ("x", "z", "y", "c"))
    both = P(("y", "c"), ("x", "z"))
    batch = P(("y", "c"))
    return jax.shard_map(
        step,
        mesh=mesh,
        in_specs=(both, both, both, batch, batch, batch, batch),
        out_specs=(both, both, P()),
        check_vma=False,
    )
```

profile of v0, /device:TPU:32, one launch (start us, length us, event | category | flops | bytes accessed | tf_op | source)
XLA Modules:
  0.0 202.2 jit_solution(9483471554947375254)
XLA Ops:
  0.6 0.8 broadcast_in_dim.18
  1.5 32.9 %all_to_all.35 = bf16[16,64,128]{2,1,0:T(8,128)(2,1)S(1)} all-to-all(bf16[16,64,128]{2,1,0:T(8,128)(2,1)S(1)} %broadcast_in_dim.18), channel_id=1, replica_groups=mesh['x'=4,'z'=16,'y'=4,'c'=2] {'z'}, dimensions={0} | all-to-all | bytes 524288 | tf_op jit(solution)/shard_map/all_to_all | solution.py:25
  34.4 1.1 broadcast_in_dim.21
  35.5 4.4 %all-to-all-start.1 = ((bf16[4,1024,128]{2,1,0:T(8,128)(2,1)}), bf16[4,1024,128]{2,1,0:T(8,128)(2,1)}, u32[]{:S(2)}, u32[]{:S(2)}) async-start(bf16[4,1024,128]{2,1,0:T(8,128)(2,1)} %broadcast_in_dim.21), calls=%async_computation.1 | async-start | bytes 2097152 | tf_op jit(solution)/shard_map/all_to_all | solution.py:25
  40.0 0.1 constant_dynamic-slice_fusion
  40.1 1.9 collective-permute-start.1
  42.0 3.5 %collective-permute-start.2 = (bf16[512,512]{1,0:T(8,128)(2,1)S(1)}, bf16[512,512]{1,0:T(8,128)(2,1)S(1)}, u32[]{:S(2)}, u32[]{:S(2)}) collective-permute-start(bf16[512,512]{1,0:T(8,128)(2,1)S(1)} %get-tuple-element.8.refs_0_), channel_id=1, source_target_pairs={{0,2},{2,4},{4,6},{6,0},{1,3},{3,5},{5,7},{7,1},{8,10},{10,12},{12... | collective-permute-start | bytes 1572872 | tf_op jit(solution)/shard_map/ppermute | solution.py:149
  45.5 3.6 %collective-permute-start.5 = (bf16[512,512]{1,0:T(8,128)(2,1)S(1)}, bf16[512,512]{1,0:T(8,128)(2,1)S(1)}, u32[]{:S(2)}, u32[]{:S(2)}) collective-permute-start(bf16[512,512]{1,0:T(8,128)(2,1)S(1)} %collective-permute-done.1.refs_1_), channel_id=1, source_target_pairs={{0,6},{2,0},{4,2},{6,4},{1,7},{3,1},{5,3},{7,5},{8,14},{10,8},{12,... | collective-permute-start | bytes 1572872 | tf_op jit(solution)/shard_map/ppermute | solution.py:152
  49.1 5.4 %all-to-all-done.1 = bf16[4,1024,128]{2,1,0:T(8,128)(2,1)} async-done(((bf16[4,1024,128]{2,1,0:T(8,128)(2,1)}), bf16[4,1024,128]{2,1,0:T(8,128)(2,1)}, u32[]{:S(2)}, u32[]{:S(2)}) %all-to-all-start.1) | async-done | bytes 1048608 | tf_op jit(solution)/shard_map/all_to_all | solution.py:25
  54.5 1.9 collective-permute-start
  56.5 4.9 %collective-permute-start.3 = (bf16[512,512]{1,0:T(8,128)(2,1)S(1)}, bf16[512,512]{1,0:T(8,128)(2,1)S(1)}, u32[]{:S(2)}, u32[]{:S(2)}) collective-permute-start(bf16[512,512]{1,0:T(8,128)(2,1)S(1)} %get-tuple-element.8.refs_0_), channel_id=1, source_target_pairs={{0,6},{2,0},{4,2},{6,4},{1,7},{3,1},{5,3},{7,5},{8,14},{10,8},{12,... | collective-permute-start | bytes 1572872 | tf_op jit(solution)/shard_map/ppermute | solution.py:150
  61.4 1.9 collective-permute-start.4
  63.3 2.5 %collective-permute-start.6 = (bf16[512,512]{1,0:T(8,128)(2,1)S(1)}, bf16[512,512]{1,0:T(8,128)(2,1)}, u32[]{:S(2)}, u32[]{:S(2)}) collective-permute-start(bf16[512,512]{1,0:T(8,128)(2,1)S(1)} %collective-permute-done.2.refs_2_), channel_id=1, source_target_pairs={{0,2},{2,4},{4,6},{6,0},{1,3},{3,5},{5,7},{7,1},{8,10},{10,12},{12... | collective-permute-start | bytes 1572872 | tf_op jit(solution)/shard_map/ppermute | solution.py:154
  65.8 4.6 %collective-permute-start.7 = (bf16[512,512]{1,0:T(8,128)(2,1)S(1)}, bf16[512,512]{1,0:T(8,128)(2,1)}, u32[]{:S(2)}, u32[]{:S(2)}) collective-permute-start(bf16[512,512]{1,0:T(8,128)(2,1)S(1)} %collective-permute-done.5.refs_5_), channel_id=1, source_target_pairs={{0,6},{2,0},{4,2},{6,4},{1,7},{3,1},{5,3},{7,5},{8,14},{10,8},{12,... | collective-permute-start | bytes 1572872 | tf_op jit(solution)/shard_map/ppermute | solution.py:155
  70.4 0.1 pad_add_fusion.place
  70.5 3.1 %collective-permute-done.3.refs_3_ = bf16[512,512]{1,0:T(8,128)(2,1)S(1)} collective-permute-done((bf16[512,512]{1,0:T(8,128)(2,1)S(1)}, bf16[512,512]{1,0:T(8,128)(2,1)S(1)}, u32[]{:S(2)}, u32[]{:S(2)}) %collective-permute-start.3) | collective-permute-done | bytes 524320 | tf_op jit(solution)/shard_map/ppermute | solution.py:150
  73.7 16.2 %collective-permute-done.6.refs_6_ = bf16[512,512]{1,0:T(8,128)(2,1)} collective-permute-done((bf16[512,512]{1,0:T(8,128)(2,1)S(1)}, bf16[512,512]{1,0:T(8,128)(2,1)}, u32[]{:S(2)}, u32[]{:S(2)}) %collective-permute-start.6) | collective-permute-done | bytes 524320 | tf_op jit(solution)/shard_map/ppermute | solution.py:154
  89.9 4.2 %forward.1 = (bf16[16,512]{1,0:T(8,128)(2,1)S(1)}, f32[256,512]{1,0:T(8,128)S(1)}) custom-call(s32[9]{0:T(128)S(1)} %pad_add_fusion.place, bf16[4096,128]{1,0:T(8,128)(2,1)} %bitcast.3.mine, bf16[4096,128]{1,0:T(8,128)(2,1)} %collective-permute-done.theirs, bf16[512,512]{1,0:T(8,128)(2,1)S(1)} %get-tuple-element.8.refs_0_, ...), custom_call_target="tpu_custom_call" | custom-call | flops 1073741824 | bytes 6815744 | tf_op jit(solution)/shard_map/forward/pallas_call | solution.py:73
  94.2 0.8 copy-done.2
  95.0 8.6 %all_to_all.36 = bf16[8,16,512]{2,1,0:T(8,128)(2,1)S(1)} all-to-all(bf16[8,16,512]{2,1,0:T(8,128)(2,1)S(1)} %broadcast_in_dim.22), channel_id=1, replica_groups=mesh['x'=4,'z'=16,'y'=4,'c'=2] {'y','c'}, dimensions={0} | all-to-all | bytes 262144 | tf_op jit(solution)/shard_map/all_to_all | solution.py:25
  103.6 0.3 fusion.6
  103.9 0.4 fusion
  104.3 0.7 broadcast_in_dim.45
  105.0 8.1 %all-to-all-start.3 = ((f32[64,4,128]{2,1,0:T(4,128)}), f32[64,4,128]{2,1,0:T(4,128)S(1)}, u32[]{:S(2)}, u32[]{:S(2)}) async-start(f32[64,4,128]{2,1,0:T(4,128)} %broadcast_in_dim.45), calls=%async_computation.3 | async-start | bytes 262144 | tf_op jit(solution)/shard_map/all_to_all | solution.py:25
  113.8 15.0 %all-to-all-done.3 = f32[64,4,128]{2,1,0:T(4,128)S(1)} async-done(((f32[64,4,128]{2,1,0:T(4,128)}), f32[64,4,128]{2,1,0:T(4,128)S(1)}, u32[]{:S(2)}, u32[]{:S(2)}) %all-to-all-start.3) | async-done | bytes 131104 | tf_op jit(solution)/shard_map/all_to_all | solution.py:25
  128.8 0.1 reduce_sum.61
  128.9 0.6 multiply_reduce_fusion
  129.5 0.4 fusion.1
  129.8 0.2 fusion.11
  130.1 0.2 convolution_add_fusion
  130.3 1.4 concatenate.11
  131.7 4.1 %all-to-all-start.4 = ((f32[8,16,640]{2,1,0:T(8,128)}), f32[8,16,640]{2,1,0:T(8,128)}, u32[]{:S(2)}, u32[]{:S(2)}) async-start(f32[8,16,640]{2,1,0:T(8,128)} %concatenate.11), calls=%async_computation.4 | async-start | bytes 655360 | tf_op jit(solution)/shard_map/all_to_all | solution.py:220
  135.8 1.8 fusion.21
  137.6 6.5 %all-to-all-done.4 = f32[8,16,640]{2,1,0:T(8,128)} async-done(((f32[8,16,640]{2,1,0:T(8,128)}), f32[8,16,640]{2,1,0:T(8,128)}, u32[]{:S(2)}, u32[]{:S(2)}) %all-to-all-start.4) | async-done | bytes 327712 | tf_op jit(solution)/shard_map/all_to_all | solution.py:220
  144.0 1.6 reduce_sum.63
  145.6 0.8 slice_bitcast_fusion
  146.4 0.9 copy-done.1
  147.3 4.2 %backward.3 = bf16[4096,128]{1,0:T(8,128)(2,1)S(1)} custom-call(s32[9]{0:T(128)S(1)} %pad_add_fusion.place, f32[8,512]{1,0:T(8,128)S(1)} %get-tuple-element.16.grad, f32[128,512]{1,0:T(8,128)S(1)} %copy-done.1, bf16[512,512]{1,0:T(8,128)(2,1)S(1)} %get-tuple-element.8.refs_0_, bf16[512,512]{1,0:T(8,128)(2,1)S(1)} %collective-permute-done.1.refs_1_, ...), custom_call_target="tpu_custom_call" | custom-call | flops 536870912 | bytes 5505024 | tf_op jit(solution)/shard_map/backward/pallas_call | solution.py:116
  151.5 1.9 collective-permute-start.8
  153.5 4.2 %backward.2 = bf16[4096,128]{1,0:T(8,128)(2,1)S(1)} custom-call(s32[9]{0:T(128)S(1)} %pad_add_fusion.place, f32[8,512]{1,0:T(8,128)S(1)} %get-tuple-element.15.grad, f32[128,512]{1,0:T(8,128)S(1)} %get-tuple-element.9.slope, bf16[512,512]{1,0:T(8,128)(2,1)S(1)} %get-tuple-element.8.refs_0_, bf16[512,512]{1,0:T(8,128)(2,1)S(1)} %collective-permute-done.1.refs_1_, ...), custom_call_target="tpu_custom_call" | custom-call | flops 536870912 | bytes 5505024 | tf_op jit(solution)/shard_map/backward/pallas_call | solution.py:116
  157.6 0.3 add_convert_fusion
  157.9 18.9 %all_to_all.37 = bf16[4,1024,128]{2,1,0:T(8,128)(2,1)S(1)} all-to-all(bf16[4,1024,128]{2,1,0:T(8,128)(2,1)S(1)} %bitcast.40), channel_id=1, replica_groups=mesh['x'=4,'z'=16,'y'=4,'c'=2] {'x'}, dimensions={0} | all-to-all | bytes 2097152 | tf_op jit(solution)/shard_map/all_to_all | solution.py:231
  176.8 0.9 reduce_sum.64
  177.7 4.5 %all-to-all-start.6 = ((bf16[16,64,128]{2,1,0:T(8,128)(2,1)}), bf16[16,64,128]{2,1,0:T(8,128)(2,1)S(1)}, u32[]{:S(2)}, u32[]{:S(2)}) async-start(bf16[16,64,128]{2,1,0:T(8,128)(2,1)} %bitcast.19), calls=%async_computation.6 | async-start | bytes 524288 | tf_op jit(solution)/shard_map/all_to_all | solution.py:233
  182.1 0.6 fusion.9
  182.7 1.2 slice.42
  184.6 15.9 %all-to-all-done.6 = bf16[16,64,128]{2,1,0:T(8,128)(2,1)S(1)} async-done(((bf16[16,64,128]{2,1,0:T(8,128)(2,1)}), bf16[16,64,128]{2,1,0:T(8,128)(2,1)S(1)}, u32[]{:S(2)}, u32[]{:S(2)}) %all-to-all-start.6) | async-done | bytes 262176 | tf_op jit(solution)/shard_map/all_to_all | solution.py:233
  200.5 0.6 reduce_sum.65
  (30 shorter events, 0.1 us)
Async XLA Ops:
  0.6 103.0 %copy-start = (bf16[256,1024]{1,0:T(8,128)(2,1)S(1)}, bf16[256,1024]{1,0:T(8,128)(2,1)}, u32[]{:S(2)}) copy-start(bf16[256,1024]{1,0:T(8,128)(2,1)} %param.11) | copy-start | bytes 1572868
  35.5 4.4 %copy-start.3 = (bf16[512,1024]{1,0:T(8,128)(2,1)S(1)}, bf16[512,1024]{1,0:T(8,128)(2,1)}, u32[]{:S(2)}) copy-start(bf16[512,1024]{1,0:T(8,128)(2,1)} %param.10) | copy-start | bytes 3145732
  35.5 19.0 %all-to-all-start.1 = ((bf16[4,1024,128]{2,1,0:T(8,128)(2,1)}), bf16[4,1024,128]{2,1,0:T(8,128)(2,1)}, u32[]{:S(2)}, u32[]{:S(2)}) async-start(bf16[4,1024,128]{2,1,0:T(8,128)(2,1)} %broadcast_in_dim.21), calls=%async_computation.1 | async-start | bytes 2097152 | tf_op jit(solution)/shard_map/all_to_all | solution.py:25
  40.0 30.5 %copy-start.5 = (s32[8]{0:T(128)S(1)}, s32[8]{0:T(128)}, u32[]{:S(2)}) copy-start(s32[8]{0:T(128)} %constant.74.clone) | copy-start | bytes 100
  40.0 30.5 %copy-start.6 = (s32[8]{0:T(128)S(1)}, s32[8]{0:T(128)}, u32[]{:S(2)}) copy-start(s32[8]{0:T(128)} %constant.75.clone) | copy-start | bytes 100
  40.1 5.4 %collective-permute-start.1 = (bf16[512,512]{1,0:T(8,128)(2,1)S(1)}, bf16[512,512]{1,0:T(8,128)(2,1)S(1)}, u32[]{:S(2)}, u32[]{:S(2)}) collective-permute-start(bf16[512,512]{1,0:T(8,128)(2,1)S(1)} %get-tuple-element.7), channel_id=1, source_target_pairs={{0,1},{1,0},{2,3},{3,2},{4,5},{5,4},{6,7},{7,6},{8,9},{9,8},{10,11... | collective-permute-start | bytes 1572872 | tf_op jit(solution)/shard_map/ppermute | solution.py:151
  42.0 21.3 %collective-permute-start.2 = (bf16[512,512]{1,0:T(8,128)(2,1)S(1)}, bf16[512,512]{1,0:T(8,128)(2,1)S(1)}, u32[]{:S(2)}, u32[]{:S(2)}) collective-permute-start(bf16[512,512]{1,0:T(8,128)(2,1)S(1)} %get-tuple-element.8.refs_0_), channel_id=1, source_target_pairs={{0,2},{2,4},{4,6},{6,0},{1,3},{3,5},{5,7},{7,1},{8,10},{10,12},{12... | collective-permute-start | bytes 1572872 | tf_op jit(solution)/shard_map/ppermute | solution.py:149
  45.5 20.3 %collective-permute-start.5 = (bf16[512,512]{1,0:T(8,128)(2,1)S(1)}, bf16[512,512]{1,0:T(8,128)(2,1)S(1)}, u32[]{:S(2)}, u32[]{:S(2)}) collective-permute-start(bf16[512,512]{1,0:T(8,128)(2,1)S(1)} %collective-permute-done.1.refs_1_), channel_id=1, source_target_pairs={{0,6},{2,0},{4,2},{6,4},{1,7},{3,1},{5,3},{7,5},{8,14},{10,8},{12,... | collective-permute-start | bytes 1572872 | tf_op jit(solution)/shard_map/ppermute | solution.py:152
  54.5 35.4 %collective-permute-start = (bf16[4096,128]{1,0:T(8,128)(2,1)}, bf16[4096,128]{1,0:T(8,128)(2,1)}, u32[]{:S(2)}, u32[]{:S(2)}) collective-permute-start(bf16[4096,128]{1,0:T(8,128)(2,1)} %bitcast.3.mine), channel_id=1, source_target_pairs={{0,1},{1,0},{2,3},{3,2},{4,5},{5,4},{6,7},{7,6},{8,9},{9,8},{10,11... | collective-permute-start | bytes 3145736 | tf_op jit(solution)/shard_map/ppermute | solution.py:159
  56.5 17.2 %collective-permute-start.3 = (bf16[512,512]{1,0:T(8,128)(2,1)S(1)}, bf16[512,512]{1,0:T(8,128)(2,1)S(1)}, u32[]{:S(2)}, u32[]{:S(2)}) collective-permute-start(bf16[512,512]{1,0:T(8,128)(2,1)S(1)} %get-tuple-element.8.refs_0_), channel_id=1, source_target_pairs={{0,6},{2,0},{4,2},{6,4},{1,7},{3,1},{5,3},{7,5},{8,14},{10,8},{12,... | collective-permute-start | bytes 1572872 | tf_op jit(solution)/shard_map/ppermute | solution.py:150
  61.4 28.5 %collective-permute-start.4 = (bf16[512,512]{1,0:T(8,128)(2,1)S(1)}, bf16[512,512]{1,0:T(8,128)(2,1)}, u32[]{:S(2)}, u32[]{:S(2)}) collective-permute-start(bf16[512,512]{1,0:T(8,128)(2,1)S(1)} %collective-permute-done.1.refs_1_), channel_id=1, source_target_pairs={{0,2},{2,4},{4,6},{6,0},{1,3},{3,5},{5,7},{7,1},{8,10},{10,12},{12... | collective-permute-start | bytes 1572872 | tf_op jit(solution)/shard_map/ppermute | solution.py:153
  63.3 26.6 %collective-permute-start.6 = (bf16[512,512]{1,0:T(8,128)(2,1)S(1)}, bf16[512,512]{1,0:T(8,128)(2,1)}, u32[]{:S(2)}, u32[]{:S(2)}) collective-permute-start(bf16[512,512]{1,0:T(8,128)(2,1)S(1)} %collective-permute-done.2.refs_2_), channel_id=1, source_target_pairs={{0,2},{2,4},{4,6},{6,0},{1,3},{3,5},{5,7},{7,1},{8,10},{10,12},{12... | collective-permute-start | bytes 1572872 | tf_op jit(solution)/shard_map/ppermute | solution.py:154
  65.8 24.1 %collective-permute-start.7 = (bf16[512,512]{1,0:T(8,128)(2,1)S(1)}, bf16[512,512]{1,0:T(8,128)(2,1)}, u32[]{:S(2)}, u32[]{:S(2)}) collective-permute-start(bf16[512,512]{1,0:T(8,128)(2,1)S(1)} %collective-permute-done.5.refs_5_), channel_id=1, source_target_pairs={{0,6},{2,0},{4,2},{6,4},{1,7},{3,1},{5,3},{7,5},{8,14},{10,8},{12,... | collective-permute-start | bytes 1572872 | tf_op jit(solution)/shard_map/ppermute | solution.py:155
  94.1 0.8 copy-start.2
  94.9 9.0 %copy-start.7 = (s32[384]{0:T(512)S(1)}, s32[384]{0:T(512)}, u32[]{:S(2)}) copy-start(s32[384]{0:T(512)} %param.13) | copy-start | bytes 4612
  94.9 9.0 %copy-start.8 = (s32[384]{0:T(512)S(1)}, s32[384]{0:T(512)}, u32[]{:S(2)}) copy-start(s32[384]{0:T(512)} %param.12) | copy-start | bytes 4612
  94.9 33.9 %copy-start.4 = (f32[384]{0:T(512)S(1)}, f32[384]{0:T(512)}, u32[]{:S(2)}) copy-start(f32[384]{0:T(512)} %param.15) | copy-start | bytes 4612
  105.0 23.8 %all-to-all-start.3 = ((f32[64,4,128]{2,1,0:T(4,128)}), f32[64,4,128]{2,1,0:T(4,128)S(1)}, u32[]{:S(2)}, u32[]{:S(2)}) async-start(f32[64,4,128]{2,1,0:T(4,128)} %broadcast_in_dim.45), calls=%async_computation.3 | async-start | bytes 262144 | tf_op jit(solution)/shard_map/all_to_all | solution.py:25
  131.7 12.3 %all-to-all-start.4 = ((f32[8,16,640]{2,1,0:T(8,128)}), f32[8,16,640]{2,1,0:T(8,128)}, u32[]{:S(2)}, u32[]{:S(2)}) async-start(f32[8,16,640]{2,1,0:T(8,128)} %concatenate.11), calls=%async_computation.4 | async-start | bytes 655360 | tf_op jit(solution)/shard_map/all_to_all | solution.py:220
  146.4 0.9 copy-start.1
  151.5 6.1 %collective-permute-start.8 = (bf16[4096,128]{1,0:T(8,128)(2,1)S(1)}, bf16[4096,128]{1,0:T(8,128)(2,1)S(1)}, u32[]{:S(2)}, u32[]{:S(2)}) collective-permute-start(bf16[4096,128]{1,0:T(8,128)(2,1)S(1)} %backward.3), channel_id=1, source_target_pairs={{0,1},{1,0},{2,3},{3,2},{4,5},{5,4},{6,7},{7,6},{8,9},{9,8},{10,11... | collective-permute-start | bytes 3145736 | tf_op jit(solution)/shard_map/ppermute | solution.py:227
  177.7 22.8 %all-to-all-start.6 = ((bf16[16,64,128]{2,1,0:T(8,128)(2,1)}), bf16[16,64,128]{2,1,0:T(8,128)(2,1)S(1)}, u32[]{:S(2)}, u32[]{:S(2)}) async-start(bf16[16,64,128]{2,1,0:T(8,128)(2,1)} %bitcast.19), calls=%async_computation.6 | async-start | bytes 524288 | tf_op jit(solution)/shard_map/all_to_all | solution.py:233
where the time goes:
time: 203 us; the launch traced here: 202 us
  waiting for transfers between devices  62.2 us (31%)
  blocking collectives  60.4 us (30%)
  starting transfers between devices  47.8 us (24%)
  Pallas kernels  12.6 us (6%)
  local copies, waits for them, and re-layouts  9.62 us (5%)
  other arithmetic  4.83 us (2%)
  between operations  3.39 us (2%)
    all_to_all x2, blocking collectives, spread(): lax.all_to_all(jnp.broadcast_to(value[None], (n,) + value.shape), axes, 0...  41.5 us
    all_to_all x2, waiting for transfers between devices, spread(): lax.all_to_all(jnp.broadcast_to(value[None], (n,) + value.shape), axes, 0...  20.5 us
    all_to_all x1, blocking collectives, step(): over_x = lax.all_to_all(hidden_terms, 'x', 0, 0, tiled=True)  18.9 us
    ppermute x1, waiting for transfers between devices, step(): far_own = lax.ppermute(prev_own, 'y', plus)  16.2 us
    all_to_all x1, waiting for transfers between devices, step(): over_z = lax.all_to_all(over_x, 'z', 0, 0, tiled=True)  15.9 us
    all_to_all x2, starting transfers between devices, spread(): lax.all_to_all(jnp.broadcast_to(value[None], (n,) + value.shape), axes, 0...  12.5 us
    pallas_call x2, Pallas kernels, backward(): pl.pallas_call(functools.partial(backward_kernel, nb), name='backward', o...  8.34 us
    all_to_all x1, waiting for transfers between devices, step(): terms = lax.all_to_all(terms, ('y', 'c'), 0, 0, tiled=True).sum(0)  6.46 us
  transfers between devices with their start and end apart: 13, of which 6 were waited for; matrix products, arithmetic and copies ran while one was open for 2% of the time, Pallas kernels for 2%

commit v1 on v0

--- a/solution.py
+++ b/solution.py
@@ -94,42 +94,163 @@
     )(place, mine, theirs, *blocks)
 
 
-def backward_kernel(nb, place, grad, slope, *refs):
-    blocks, (out, held, sems) = refs[:nb], refs[nb:]
-    rows = held.shape[1]
-    copies = [pltpu.make_async_copy(blocks[k], held.at[k], sems.at[k]) for k in range(nb)]
-    for copy in copies:
-        copy.start()
+def scores_kernel(place, every, passages, pair_query, pair_passage, out, pooled):
+    groups, queries, half = every.shape
+    cores = passages.shape[1] // half
+    c, y = place[place.shape[0] - 2], place[place.shape[0] - 1]
+    table = None
+    for i in range(cores):
+        columns = pl.ds(i * half, half)
+        part = jnp.concatenate([every[g] for g in range(i, groups, cores)], axis=0)
+        term = dot(passages[:, columns], part, 1, 1)
+        table = term if table is None else table + term
+        here = every[y * cores + i].astype(F32)
+        kept = queries // cores
+        pooled[:, columns] = jnp.where(c == 1, here[kept:], here[:kept]).astype(BF16)
+    n_passage, n_query = table.shape
+    slots = pair_query.shape[1]
+    query_hot = pair_query[...] == lax.broadcasted_iota(jnp.int32, (n_query, slots), 0)
+    passage_hot = pair_passage[...] == lax.broadcasted_iota(jnp.int32, (n_passage, slots), 0)
+    spread_table = lax.dot_general(
+        table,
+        query_hot.astype(F32),
+        (((1,), (0,)), ((), ())),
+        precision=lax.Precision.HIGHEST,
+        preferred_element_type=F32,
+    )
+    value = jnp.where(passage_hot, spread_table, 0.0).sum(0, keepdims=True)
+    out[...] = jnp.broadcast_to(value[None], out.shape)
+
+
+def pair_scores(place, every, passages, pair_query, pair_passage, peers):
+    slots = pair_query.shape[1]
+    _, queries, half = every.shape
+    cores = passages.shape[1] // half
+    return pl.pallas_call(
+        scores_kernel,
+        name="pair_scores",
+        out_shape=(
+            jax.ShapeDtypeStruct((peers, 1, slots), F32),
+            jax.ShapeDtypeStruct((queries // cores, cores * half), BF16),
+        ),
+        in_specs=[SMEM] + [WHOLE] * 4,
+        out_specs=(WHOLE, WHOLE),
+        compiler_params=pltpu.CompilerParams(vmem_limit_bytes=16 << 20),
+    )(place, every, passages, pair_query, pair_passage)
+
+
+def terms_kernel(pair_count, partials, teacher, pair_query, pair_passage, passages, out):
+    groups, queries, width = out.shape
+    half = width - LANES
+    cores = passages.shape[1] // half
+    slots = pair_query.shape[1]
+    inv_root = 1.0 / math.sqrt(VOCAB)
+    scores = partials[...].sum(0) * inv_root
+    is_live = lax.broadcasted_iota(jnp.int32, (1, slots), 1) < pair_count[0]
+    residual = jnp.where(is_live, scores - teacher[...], 0.0)
+    error = jnp.sum(residual * residual)
+    pair_grad = 2.0 * residual * inv_root
+    n_query, n_passage = queries * groups // cores, passages.shape[0]
+    query_hot = pair_query[...] == lax.broadcasted_iota(jnp.int32, (n_query, slots), 0)
+    passage_hot = pair_passage[...] == lax.broadcasted_iota(jnp.int32, (n_passage, slots), 0)
+    table = lax.dot_general(
+        query_hot.astype(F32),
+        jnp.where(passage_hot, pair_grad, 0.0),
+        (((1,), (1,)), ((), ())),
+        precision=lax.Precision.HIGHEST,
+        preferred_element_type=F32,
+    )
+    high = table.astype(BF16)
+    low = (table - high.astype(F32)).astype(BF16)
+    parts = jnp.concatenate([high, low], axis=0)
+    for i in range(cores):
+        both = dot(parts, passages[:, i * half : (i + 1) * half], 1, 0)
+        terms = both[:n_query] + both[n_query:]
+        for k in range(groups // cores):
+            out[k * cores + i, :, :half] = terms[k * queries : (k + 1) * queries]
+    out[:, :, half:] = jnp.full((groups, queries, LANES), error, F32)
+
+
+def query_terms(pair_count, partials, teacher, pair_query, pair_passage, passages, shape):
+    return pl.pallas_call(
+        terms_kernel,
+        name="query_terms",
+        out_shape=jax.ShapeDtypeStruct(shape, F32),
+        in_specs=[SMEM] + [WHOLE] * 5,
+        out_specs=WHOLE,
+        compiler_params=pltpu.CompilerParams(vmem_limit_bytes=16 << 20),
+    )(pair_count, partials, teacher, pair_query, pair_passage, passages)
+
+
+PARTS = 2
+
+
+def multiply(place, part, blocks, held, sems, logit_grad, mine, theirs):
+    nb = len(blocks)
+    rows = held.shape[1] * held.shape[2]
+    tok = mine.shape[1]
+    for k in range(nb):
+        pltpu.make_async_copy(blocks[k].at[:, part], held.at[k], sems.at[k]).wait()
+        start = pl.multiple_of(place[k] // PARTS, rows)
+        block = held[k].reshape(rows, held.shape[3])
+        term = dot(block, logit_grad, 1, 1).astype(BF16)
+        mine[pl.ds(start, rows), :] = term[:, :tok]
+        theirs[pl.ds(start, rows), :] = term[:, tok:]
+
+
+def first_kernel(nb, place, terms, slope, *refs):
+    blocks, (mine, theirs, grads, loss, held, sems) = refs[:nb], refs[nb:]
+    for k in range(nb):
+        pltpu.make_async_copy(blocks[k].at[:, 0], held.at[k], sems.at[k]).start()
     tok, cols = slope.shape
-    spread_grad = jnp.broadcast_to(grad[...][:, None, :], (tok // QLEN, QLEN, cols))
-    logit_grad = (spread_grad.reshape(tok, cols) * slope[...]).astype(BF16)
+    total = terms[...].sum(0)
+    loss[...] = total[:1, cols:]
+    half = total.shape[0] // 2
+    swapped = place[nb] == 1
+    one, two = total[:half, :cols], total[half:, :cols]
+    kept = jnp.concatenate([jnp.where(swapped, two, one), jnp.where(swapped, one, two)], axis=0)
+    wide = jnp.broadcast_to(kept[:, None, :], (tok // QLEN, QLEN, cols)).reshape(tok, cols)
+    grads[...] = (wide * slope[...]).astype(BF16)
+    multiply(place, 0, blocks, held, sems, grads[...], mine, theirs)
+
+
+def next_kernel(nb, part, place, grads, *refs):
+    blocks, (mine, theirs, held, sems) = refs[:nb], refs[nb:]
     for k in range(nb):
-        copies[k].wait()
-        start = pl.multiple_of(place[k], rows)
-        out[pl.ds(start, rows), :] = dot(held[k], logit_grad, 1, 1).astype(BF16)
-
-
-def backward(place, grad, slope, blocks):
-    nb, (rows, cols) = len(blocks), blocks[0].shape
-    tok = slope.shape[0]
-    depth = nb * rows
+        pltpu.make_async_copy(blocks[k].at[:, part], held.at[k], sems.at[k]).start()
+    multiply(place, part, blocks, held, sems, grads[...], mine, theirs)
+
+
+def backward_call(part, place, given, blocks):
+    nb = len(blocks)
+    lead, _, rows, cols = blocks[0].shape
+    tok = given[-1].shape[0] // 2
+    depth = nb * lead * rows
+    shapes = [jax.ShapeDtypeStruct((depth, tok), BF16)] * 2
+    if part == 0:
+        shapes += [
+            jax.ShapeDtypeStruct((2 * tok, cols), BF16),
+            jax.ShapeDtypeStruct((1, LANES), F32),
+        ]
+    body = functools.partial(first_kernel, nb)
+    if part:
+        body = functools.partial(next_kernel, nb, part)
     return pl.pallas_call(
-        functools.partial(backward_kernel, nb),
-        name="backward",
-        out_shape=jax.ShapeDtypeStruct((depth, tok), BF16),
-        in_specs=[SMEM, WHOLE, WHOLE] + [ANY] * nb,
-        out_specs=WHOLE,
+        body,
+        out_shape=tuple(shapes),
+        in_specs=[SMEM] + [WHOLE] * len(given) + [ANY] * nb,
+        out_specs=(WHOLE,) * len(shapes),
         scratch_shapes=[
-            pltpu.VMEM((nb, rows, cols), BF16),
+            pltpu.VMEM((nb, lead, rows, cols), BF16),
             pltpu.SemaphoreType.DMA((nb,)),
         ],
         cost_estimate=pl.CostEstimate(
-            flops=2 * tok * depth * cols,
-            bytes_accessed=2 * depth * (tok + cols) + 4 * tok * cols,
+            flops=4 * tok * depth * cols,
+            bytes_accessed=2 * depth * (2 * tok + cols) + 4 * tok * cols,
             transcendentals=0,
         ),
         compiler_params=pltpu.CompilerParams(vmem_limit_bytes=32 << 20),
-    )(place, grad, slope, *blocks)
+    )(place, *given, *blocks)
 
 
 def step(hidden, head, passages, pair_query, pair_passage, pair_count, teacher):
@@ -172,66 +293,45 @@
     steps = jnp.array([step for step, _, _ in held], jnp.int32)
     others = jnp.array([other for _, other, _ in held], jnp.int32)
     owner = ((y + steps) % ny) * nc + (c + others) % nc
-    place = jnp.concatenate([owner * rows, c[None]]).astype(jnp.int32)
+    place = jnp.concatenate([owner * rows, c[None], y[None]]).astype(jnp.int32)
 
     both, slope = forward(place, mine, theirs, blocks)
-    every = spread(both, ("y", "c"), batch).reshape(ny, nc, nc * queries, half)
-    halves = [every[:, i].reshape(batch * queries, half) for i in range(nc)]
-    wide = jnp.concatenate(halves, axis=1)
-    pooled = lax.dynamic_slice_in_dim(wide, (y * nc + c) * queries, queries, 0)
-
-    inv_root = 1.0 / math.sqrt(VOCAB)
+    every = spread(both, ("y", "c"), batch)
+
     slots = pair_query.shape[0]
-    n_query, n_passage = batch * queries, passages.shape[0]
-    table = dot(passages, wide, 1, 1)
-    query_hot = (pair_query[None, :] == jnp.arange(n_query, dtype=jnp.int32)[:, None]).astype(F32)
-    passage_hot = (
-        pair_passage[None, :] == jnp.arange(n_passage, dtype=jnp.int32)[:, None]
-    ).astype(F32)
-    spread_table = jnp.dot(table, query_hot, precision=lax.Precision.HIGHEST)
-    partial_value = (spread_table * passage_hot).sum(0)
-    packed = jnp.pad(partial_value, (0, -slots % 512)).reshape(-1, LANES)
-    packed = spread(packed, ("x", "z"), nx * nz).sum(0)
-    scores = packed.reshape(-1)[:slots] * inv_root
-
-    is_live = jnp.arange(slots, dtype=jnp.int32) < pair_count[0]
-    residual = jnp.where(is_live, scores - teacher, 0.0)
-    error = jnp.sum(residual * residual)
-    pair_grad = 2.0 * residual * inv_root
-    pair_table = lax.dot_general(
-        query_hot,
-        passage_hot * pair_grad[None, :],
-        (((1,), (1,)), ((), ())),
-        precision=lax.Precision.HIGHEST,
+    pair_query, pair_passage = pair_query.reshape(1, slots), pair_passage.reshape(1, slots)
+    partials, pooled = pair_scores(place, every, passages, pair_query, pair_passage, nx * nz)
+    partials = lax.all_to_all(partials, ("x", "z"), 0, 0, tiled=True)
+    terms = query_terms(
+        pair_count,
+        partials,
+        teacher.reshape(1, slots),
+        pair_query,
+        pair_passage,
+        passages,
+        (batch, nc * queries, half + LANES),
     )
-    table_high = pair_table.astype(BF16)
-    table_low = (pair_table - table_high.astype(F32)).astype(BF16)
-    query_terms = dot(table_high, passages, 1, 0) + dot(table_low, passages, 1, 0)
-    terms = jnp.stack(
-        [
-            query_terms[:, i * half : (i + 1) * half].reshape(ny, nc * queries, half)
-            for i in range(nc)
-        ],
-        axis=1,
-    ).reshape(batch, nc * queries, half)
-    terms = jnp.concatenate(
-        [terms, jnp.broadcast_to(error, (batch, nc * queries, LANES))], axis=2
-    )
-    terms = lax.all_to_all(terms, ("y", "c"), 0, 0, tiled=True).sum(0)
-    loss_value = terms[0, half] / (slots * batch)
-    grads = terms[:, :half].reshape(nc, queries, half)
-    grad_mine = lax.dynamic_index_in_dim(grads, c, 0, keepdims=False)
-    grad_theirs = lax.dynamic_index_in_dim(grads, 1 - c, 0, keepdims=False)
-
-    terms_theirs = backward(place, grad_theirs, slope[tok:], blocks)
-    terms_pair = lax.ppermute(terms_theirs, "c", swap)
-    terms_mine = backward(place, grad_mine, slope[:tok], blocks)
-    hidden_terms = (terms_mine.astype(F32) + terms_pair.astype(F32)).astype(BF16)
-    hidden_terms = hidden_terms.reshape(nx, nz * feat, tok)
-    over_x = lax.all_to_all(hidden_terms, "x", 0, 0, tiled=True)
-    over_x = over_x.astype(F32).sum(0).astype(BF16).reshape(nz, feat, tok)
-    over_z = lax.all_to_all(over_x, "z", 0, 0, tiled=True)
-    grad_hidden = over_z.astype(F32).sum(0).astype(BF16).T
+    terms = lax.all_to_all(terms, ("y", "c"), 0, 0, tiled=True)
+
+    sliced = [block.reshape(rows // feat, PARTS, feat // PARTS, half) for block in blocks]
+    given = (terms, slope)
+    sums = []
+    for part in range(PARTS):
+        results = backward_call(part, place, given, sliced)
+        if part == 0:
+            given = (results[2],)
+            loss_value = results[3][0, 0] / (slots * batch)
+        other = lax.ppermute(results[1], "c", swap)
+        sums.append((results[0], other))
+    slices = []
+    for part, (kept, other) in enumerate(sums):
+        shape = (nx, nz * feat // PARTS, tok)
+        hidden_terms = (kept.astype(F32) + other.astype(F32)).astype(BF16).reshape(shape)
+        over_x = lax.all_to_all(hidden_terms, "x", 0, 0, tiled=True)
+        over_x = over_x.astype(F32).sum(0).astype(BF16).reshape(nz, feat // PARTS, tok)
+        over_z = lax.all_to_all(over_x, "z", 0, 0, tiled=True)
+        slices.append(over_z.astype(F32).sum(0).astype(BF16))
+    grad_hidden = jnp.concatenate(slices, axis=0).T
     return (pooled, grad_hidden, loss_value)
 
 

time: 203 us -> 220 us (1.084)
  waiting for transfers between devices: 62.2 us -> 85 us
  blocking collectives: 60.4 us -> 43.6 us
  starting transfers between devices: 47.8 us -> 61.4 us
  local copies, waits for them, and re-layouts: 9.62 us -> 6.86 us
    all_to_all x1 -> x3, waiting for transfers between devices: 6.46 us -> 31.2 us  [the longest x2 17.2 us: step(): over_x = lax.all_to_all(hidden_terms, 'x', 0, 0, tiled=True)]
    all_to_all x1 -> x3, starting transfers between devices: 4.07 us -> 15.3 us  [the longest x1 8.26 us: step(): partials = lax.all_to_all(partials, ('x', 'z'), 0, 0, tiled=True)]
    all_to_all x2, waiting for transfers between devices: 20.5 us -> 10.8 us  [spread(): lax.all_to_all(jnp.broadcast_to(value[None], (n,) + value.shape), axes, 0...]
    all_to_all x2 -> x1, blocking collectives: 41.5 us -> 32.9 us  [spread(): lax.all_to_all(jnp.broadcast_to(value[None], (n,) + value.shape), axes, 0...]
    all_to_all x1 -> x2, waiting for transfers between devices: 15.9 us -> 24.3 us  [step(): over_z = lax.all_to_all(over_x, 'z', 0, 0, tiled=True)]
    all_to_all x1, blocking collectives: 18.9 us -> 10.7 us  [step(): terms = lax.all_to_all(terms, ('y', 'c'), 0, 0, tiled=True)]
    all_to_all x2, starting transfers between devices: 12.5 us -> 7.93 us  [spread(): lax.all_to_all(jnp.broadcast_to(value[None], (n,) + value.shape), axes, 0...]
    all_to_all x1 -> x2, starting transfers between devices: 4.46 us -> 9.04 us  [step(): over_z = lax.all_to_all(over_x, 'z', 0, 0, tiled=True)]
  transfers between devices with their start and end apart: 13 -> 17, of which waited for: 6 -> 9; matrix products, arithmetic and copies ran while one was open for 2% -> 2% of each run, Pallas kernels for 2% -> 2%
where the time goes in v1:
time: 220 us; the launch traced here: 218 us
  waiting for transfers between devices  85 us (39%)
  starting transfers between devices  61.4 us (28%)
  blocking collectives  43.6 us (20%)
  Pallas kernels  14.6 us (7%)
  local copies, waits for them, and re-layouts  6.86 us (3%)
  other arithmetic  4.14 us (2%)
  between operations  2.76 us (1%)
    all_to_all x1, blocking collectives, spread(): lax.all_to_all(jnp.broadcast_to(value[None], (n,) + value.shape), axes, 0...  32.9 us
    all_to_all x2, waiting for transfers between devices, step(): over_z = lax.all_to_all(over_x, 'z', 0, 0, tiled=True)  24.3 us
    all_to_all x2, waiting for transfers between devices, step(): over_x = lax.all_to_all(hidden_terms, 'x', 0, 0, tiled=True)  17.2 us
    ppermute x1, waiting for transfers between devices, step(): far_own = lax.ppermute(prev_own, 'y', plus)  16.2 us
    all_to_all x1, waiting for transfers between devices, step(): partials = lax.all_to_all(partials, ('x', 'z'), 0, 0, tiled=True)  14 us
    all_to_all x2, waiting for transfers between devices, spread(): lax.all_to_all(jnp.broadcast_to(value[None], (n,) + value.shape), axes, 0...  10.8 us
    all_to_all x1, blocking collectives, step(): terms = lax.all_to_all(terms, ('y', 'c'), 0, 0, tiled=True)  10.7 us
    all_to_all x2, starting transfers between devices, step(): over_z = lax.all_to_all(over_x, 'z', 0, 0, tiled=True)  9.04 us
  transfers between devices with their start and end apart: 17, of which 9 were waited for; matrix products, arithmetic and copies ran while one was open for 2% of the time, Pallas kernels for 2%

profile of v1, /device:TPU:32, one launch (start us, length us, event | category | flops | bytes accessed | tf_op | source)
XLA Modules:
  0.0 218.4 jit_solution(13871171421222291643)
XLA Ops:
  0.6 0.8 broadcast_in_dim.27
  1.4 32.9 %all_to_all.45 = bf16[16,64,128]{2,1,0:T(8,128)(2,1)S(1)} all-to-all(bf16[16,64,128]{2,1,0:T(8,128)(2,1)S(1)} %broadcast_in_dim.27), channel_id=1, replica_groups=mesh['x'=4,'z'=16,'y'=4,'c'=2] {'z'}, dimensions={0} | all-to-all | bytes 524288 | tf_op jit(solution)/shard_map/all_to_all | solution.py:25
  34.3 1.1 broadcast_in_dim.29
  35.4 4.4 %all-to-all-start.1 = ((bf16[4,1024,128]{2,1,0:T(8,128)(2,1)}), bf16[4,1024,128]{2,1,0:T(8,128)(2,1)}, u32[]{:S(2)}, u32[]{:S(2)}) async-start(bf16[4,1024,128]{2,1,0:T(8,128)(2,1)} %broadcast_in_dim.29), calls=%async_computation.1 | async-start | bytes 2097152 | tf_op jit(solution)/shard_map/all_to_all | solution.py:25
  39.8 0.1 constant_dynamic-slice_fusion
  39.9 1.9 collective-permute-start.1
  41.9 3.5 %collective-permute-start.2 = (bf16[512,512]{1,0:T(8,128)(2,1)S(1)}, bf16[512,512]{1,0:T(8,128)(2,1)S(1)}, u32[]{:S(2)}, u32[]{:S(2)}) collective-permute-start(bf16[512,512]{1,0:T(8,128)(2,1)S(1)} %get-tuple-element.24.refs_0_), channel_id=1, source_target_pairs={{0,2},{2,4},{4,6},{6,0},{1,3},{3,5},{5,7},{7,1},{8,10},{10,12},{12... | collective-permute-start | bytes 1572872 | tf_op jit(solution)/shard_map/ppermute | solution.py:270
  45.4 3.6 %collective-permute-start.5 = (bf16[512,512]{1,0:T(8,128)(2,1)S(1)}, bf16[512,512]{1,0:T(8,128)(2,1)S(1)}, u32[]{:S(2)}, u32[]{:S(2)}) collective-permute-start(bf16[512,512]{1,0:T(8,128)(2,1)S(1)} %collective-permute-done.1.refs_1_), channel_id=1, source_target_pairs={{0,6},{2,0},{4,2},{6,4},{1,7},{3,1},{5,3},{7,5},{8,14},{10,8},{12,... | collective-permute-start | bytes 1572872 | tf_op jit(solution)/shard_map/ppermute | solution.py:273
  49.0 5.5 %all-to-all-done.1 = bf16[4,1024,128]{2,1,0:T(8,128)(2,1)} async-done(((bf16[4,1024,128]{2,1,0:T(8,128)(2,1)}), bf16[4,1024,128]{2,1,0:T(8,128)(2,1)}, u32[]{:S(2)}, u32[]{:S(2)}) %all-to-all-start.1) | async-done | bytes 1048608 | tf_op jit(solution)/shard_map/all_to_all | solution.py:25
  54.4 1.9 collective-permute-start
  56.3 4.9 %collective-permute-start.3 = (bf16[512,512]{1,0:T(8,128)(2,1)S(1)}, bf16[512,512]{1,0:T(8,128)(2,1)S(1)}, u32[]{:S(2)}, u32[]{:S(2)}) collective-permute-start(bf16[512,512]{1,0:T(8,128)(2,1)S(1)} %get-tuple-element.24.refs_0_), channel_id=1, source_target_pairs={{0,6},{2,0},{4,2},{6,4},{1,7},{3,1},{5,3},{7,5},{8,14},{10,8},{12,... | collective-permute-start | bytes 1572872 | tf_op jit(solution)/shard_map/ppermute | solution.py:271
  61.3 1.9 collective-permute-start.4
  63.2 2.5 %collective-permute-start.6 = (bf16[512,512]{1,0:T(8,128)(2,1)S(1)}, bf16[512,512]{1,0:T(8,128)(2,1)}, u32[]{:S(2)}, u32[]{:S(2)}) collective-permute-start(bf16[512,512]{1,0:T(8,128)(2,1)S(1)} %collective-permute-done.2.refs_2_), channel_id=1, source_target_pairs={{0,2},{2,4},{4,6},{6,0},{1,3},{3,5},{5,7},{7,1},{8,10},{10,12},{12... | collective-permute-start | bytes 1572872 | tf_op jit(solution)/shard_map/ppermute | solution.py:275
  65.7 4.6 %collective-permute-start.7 = (bf16[512,512]{1,0:T(8,128)(2,1)S(1)}, bf16[512,512]{1,0:T(8,128)(2,1)}, u32[]{:S(2)}, u32[]{:S(2)}) collective-permute-start(bf16[512,512]{1,0:T(8,128)(2,1)S(1)} %collective-permute-done.5.refs_5_), channel_id=1, source_target_pairs={{0,6},{2,0},{4,2},{6,4},{1,7},{3,1},{5,3},{7,5},{8,14},{10,8},{12,... | collective-permute-start | bytes 1572872 | tf_op jit(solution)/shard_map/ppermute | solution.py:276
  70.3 0.6 copy-done.10
  71.0 0.1 pad_add_fusion.place
  71.1 2.5 %collective-permute-done.3.refs_3_ = bf16[512,512]{1,0:T(8,128)(2,1)S(1)} collective-permute-done((bf16[512,512]{1,0:T(8,128)(2,1)S(1)}, bf16[512,512]{1,0:T(8,128)(2,1)S(1)}, u32[]{:S(2)}, u32[]{:S(2)}) %collective-permute-start.3) | collective-permute-done | bytes 524320 | tf_op jit(solution)/shard_map/ppermute | solution.py:271
  73.6 16.2 %collective-permute-done.6.refs_6_ = bf16[512,512]{1,0:T(8,128)(2,1)} collective-permute-done((bf16[512,512]{1,0:T(8,128)(2,1)S(1)}, bf16[512,512]{1,0:T(8,128)(2,1)}, u32[]{:S(2)}, u32[]{:S(2)}) %collective-permute-start.6) | collective-permute-done | bytes 524320 | tf_op jit(solution)/shard_map/ppermute | solution.py:275
  89.8 4.2 %forward.1 = (bf16[16,512]{1,0:T(8,128)(2,1)S(1)}, f32[256,512]{1,0:T(8,128)S(1)}) custom-call(s32[10]{0:T(128)S(1)} %pad_add_fusion.place, bf16[4096,128]{1,0:T(8,128)(2,1)} %bitcast.4.mine, bf16[4096,128]{1,0:T(8,128)(2,1)} %collective-permute-done.theirs, bf16[512,512]{1,0:T(8,128)(2,1)S(1)} %get-tuple-element.24.refs_0_, ...), custom_call_target="tpu_custom_call" | custom-call | flops 1073741824 | bytes 6815744 | tf_op jit(solution)/shard_map/forward/pallas_call | solution.py:73
  94.0 0.8 copy-done.4
  94.8 0.7 broadcast_in_dim.30
  95.5 3.5 %all-to-all-start.2 = ((bf16[8,16,512]{2,1,0:T(8,128)(2,1)}), bf16[8,16,512]{2,1,0:T(8,128)(2,1)S(1)}, u32[]{:S(2)}, u32[]{:S(2)}) async-start(bf16[8,16,512]{2,1,0:T(8,128)(2,1)} %broadcast_in_dim.30), calls=%async_computation.2 | async-start | bytes 262144 | tf_op jit(solution)/shard_map/all_to_all | solution.py:25
  99.0 0.7 copy-done.8
  99.7 5.3 %all-to-all-done.2.every = bf16[8,16,512]{2,1,0:T(8,128)(2,1)S(1)} async-done(((bf16[8,16,512]{2,1,0:T(8,128)(2,1)}), bf16[8,16,512]{2,1,0:T(8,128)(2,1)S(1)}, u32[]{:S(2)}, u32[]{:S(2)}) %all-to-all-start.2) | async-done | bytes 131104 | tf_op jit(solution)/shard_map/all_to_all | solution.py:25
  105.0 1.0 copy-done
  106.1 2.0 pair_scores.1
  108.1 8.3 %all-to-all-start.3 = ((f32[64,1,384]{2,1,0:T(1,128)}), f32[64,1,384]{2,1,0:T(1,128)S(1)}, u32[]{:S(2)}, u32[]{:S(2)}) async-start(f32[64,1,384]{2,1,0:T(1,128)} %get-tuple-element.15), calls=%async_computation.3 | async-start | bytes 196608 | tf_op jit(solution)/shard_map/all_to_all | solution.py:304
  117.1 14.0 %all-to-all-done.3.partials = f32[64,1,384]{2,1,0:T(1,128)S(1)} async-done(((f32[64,1,384]{2,1,0:T(1,128)}), f32[64,1,384]{2,1,0:T(1,128)S(1)}, u32[]{:S(2)}, u32[]{:S(2)}) %all-to-all-start.3) | async-done | bytes 98336 | tf_op jit(solution)/shard_map/all_to_all | solution.py:304
  131.0 1.0 copy-done.1
  132.1 0.9 query_terms.1
  133.0 10.7 %all_to_all.46.terms = f32[8,16,640]{2,1,0:T(8,128)S(1)} all-to-all(f32[8,16,640]{2,1,0:T(8,128)S(1)} %query_terms.1), channel_id=1, replica_groups=mesh['x'=4,'z'=16,'y'=4,'c'=2] {'y','c'}, dimensions={0} | all-to-all | bytes 655360 | tf_op jit(solution)/shard_map/all_to_all | solution.py:314
  143.7 3.3 %shard_map.112 = (bf16[2048,128]{1,0:T(8,128)(2,1)S(1)}, bf16[2048,128]{1,0:T(8,128)(2,1)S(1)}, bf16[256,512]{1,0:T(8,128)(2,1)S(1)}, f32[1,128]{1,0:T(1,128)S(1)}) custom-call(s32[10]{0:T(128)S(1)} %pad_add_fusion.place, f32[8,16,640]{2,1,0:T(8,128)S(1)} %all_to_all.46.terms, f32[256,512]{1,0:T(8,128)S(1)} %copy-done.5, ...), custom_call_target="tpu_custom_call" | custom-call | flops 536870912 | bytes 3407872 | tf_op jit(solution)/shard_map/pallas_call | solution.py:238
  147.0 1.9 collective-permute-start.8
  149.0 4.1 %shard_map.113 = (bf16[2048,128]{1,0:T(8,128)(2,1)S(1)}, bf16[2048,128]{1,0:T(8,128)(2,1)}) custom-call(s32[10]{0:T(128)S(1)} %pad_add_fusion.place, bf16[256,512]{1,0:T(8,128)(2,1)S(1)} %get-tuple-element.19.grads, bf16[8,2,32,512]{3,2,1,0:T(8,128)(2,1)S(1)} %bitcast.22, bf16[8,2,32,512]{3,2,1,0:T(8,128)(2,1)S(1)} %bitcast.24, ...), custom_call_target="tpu_custom_call" | custom-call | flops 536870912 | bytes 3407872 | tf_op jit(solution)/shard_map/pallas_call | solution.py:238
  153.1 2.4 %collective-permute-start.9 = (bf16[2048,128]{1,0:T(8,128)(2,1)}, bf16[2048,128]{1,0:T(8,128)(2,1)S(1)}, u32[]{:S(2)}, u32[]{:S(2)}) collective-permute-start(bf16[2048,128]{1,0:T(8,128)(2,1)} %get-tuple-element.21), channel_id=1, source_target_pairs={{0,1},{1,0},{2,3},{3,2},{4,5},{5,4},{6,7},{7,6},{8,9},{9,8},{10,11... | collective-permute-start | bytes 1572872 | tf_op jit(solution)/shard_map/ppermute | solution.py:324
  155.5 1.0 add_convert_fusion.1
  156.5 3.6 %all-to-all-start.5 = ((bf16[4,512,128]{2,1,0:T(8,128)(2,1)}), bf16[4,512,128]{2,1,0:T(8,128)(2,1)S(1)}, u32[]{:S(2)}, u32[]{:S(2)}) async-start(bf16[4,512,128]{2,1,0:T(8,128)(2,1)} %bitcast.13), calls=%async_computation.5 | async-start | bytes 1048576 | tf_op jit(solution)/shard_map/all_to_all | solution.py:330
  160.1 0.9 add_convert_fusion
  161.0 8.9 %all-to-all-done.5 = bf16[4,512,128]{2,1,0:T(8,128)(2,1)S(1)} async-done(((bf16[4,512,128]{2,1,0:T(8,128)(2,1)}), bf16[4,512,128]{2,1,0:T(8,128)(2,1)S(1)}, u32[]{:S(2)}, u32[]{:S(2)}) %all-to-all-start.5) | async-done | bytes 524320 | tf_op jit(solution)/shard_map/all_to_all | solution.py:330
  170.0 3.5 %all-to-all-start.7 = ((bf16[4,512,128]{2,1,0:T(8,128)(2,1)}), bf16[4,512,128]{2,1,0:T(8,128)(2,1)S(1)}, u32[]{:S(2)}, u32[]{:S(2)}) async-start(bf16[4,512,128]{2,1,0:T(8,128)(2,1)} %bitcast.15), calls=%async_computation.7 | async-start | bytes 1048576 | tf_op jit(solution)/shard_map/all_to_all | solution.py:330
  173.4 0.7 reduce_sum.48
  174.2 8.3 %all-to-all-done.7 = bf16[4,512,128]{2,1,0:T(8,128)(2,1)S(1)} async-done(((bf16[4,512,128]{2,1,0:T(8,128)(2,1)}), bf16[4,512,128]{2,1,0:T(8,128)(2,1)S(1)}, u32[]{:S(2)}, u32[]{:S(2)}) %all-to-all-start.7) | async-done | bytes 524320 | tf_op jit(solution)/shard_map/all_to_all | solution.py:330
  182.5 4.4 %all-to-all-start.6 = ((bf16[16,32,128]{2,1,0:T(8,128)(2,1)}), bf16[16,32,128]{2,1,0:T(8,128)(2,1)S(1)}, u32[]{:S(2)}, u32[]{:S(2)}) async-start(bf16[16,32,128]{2,1,0:T(8,128)(2,1)} %bitcast.14), calls=%async_computation.6 | async-start | bytes 262144 | tf_op jit(solution)/shard_map/all_to_all | solution.py:332
  186.9 0.7 reduce_sum.50
  187.6 11.8 %all-to-all-done.6 = bf16[16,32,128]{2,1,0:T(8,128)(2,1)S(1)} async-done(((bf16[16,32,128]{2,1,0:T(8,128)(2,1)}), bf16[16,32,128]{2,1,0:T(8,128)(2,1)S(1)}, u32[]{:S(2)}, u32[]{:S(2)}) %all-to-all-start.6) | async-done | bytes 131104 | tf_op jit(solution)/shard_map/all_to_all | solution.py:332
  199.5 4.6 %all-to-all-start.8 = ((bf16[16,32,128]{2,1,0:T(8,128)(2,1)}), bf16[16,32,128]{2,1,0:T(8,128)(2,1)S(1)}, u32[]{:S(2)}, u32[]{:S(2)}) async-start(bf16[16,32,128]{2,1,0:T(8,128)(2,1)} %bitcast.16), calls=%async_computation.8 | async-start | bytes 262144 | tf_op jit(solution)/shard_map/all_to_all | solution.py:332
  204.2 12.5 %all-to-all-done.8 = bf16[16,32,128]{2,1,0:T(8,128)(2,1)S(1)} async-done(((bf16[16,32,128]{2,1,0:T(8,128)(2,1)}), bf16[16,32,128]{2,1,0:T(8,128)(2,1)S(1)}, u32[]{:S(2)}, u32[]{:S(2)}) %all-to-all-start.8) | async-done | bytes 131104 | tf_op jit(solution)/shard_map/all_to_all | solution.py:332
  216.7 0.6 maximum_bitcast_fusion
  (33 shorter events, 0.2 us)
Async XLA Ops:
  35.4 4.4 %copy-start.6 = (bf16[512,1024]{1,0:T(8,128)(2,1)S(1)}, bf16[512,1024]{1,0:T(8,128)(2,1)}, u32[]{:S(2)}) copy-start(bf16[512,1024]{1,0:T(8,128)(2,1)} %param.10) | copy-start | bytes 3145732
  35.4 19.0 %all-to-all-start.1 = ((bf16[4,1024,128]{2,1,0:T(8,128)(2,1)}), bf16[4,1024,128]{2,1,0:T(8,128)(2,1)}, u32[]{:S(2)}, u32[]{:S(2)}) async-start(bf16[4,1024,128]{2,1,0:T(8,128)(2,1)} %broadcast_in_dim.29), calls=%async_computation.1 | async-start | bytes 2097152 | tf_op jit(solution)/shard_map/all_to_all | solution.py:25
  39.9 5.4 %collective-permute-start.1 = (bf16[512,512]{1,0:T(8,128)(2,1)S(1)}, bf16[512,512]{1,0:T(8,128)(2,1)S(1)}, u32[]{:S(2)}, u32[]{:S(2)}) collective-permute-start(bf16[512,512]{1,0:T(8,128)(2,1)S(1)} %get-tuple-element.23), channel_id=1, source_target_pairs={{0,1},{1,0},{2,3},{3,2},{4,5},{5,4},{6,7},{7,6},{8,9},{9,8},{10,11... | collective-permute-start | bytes 1572872 | tf_op jit(solution)/shard_map/ppermute | solution.py:272
  41.9 21.3 %collective-permute-start.2 = (bf16[512,512]{1,0:T(8,128)(2,1)S(1)}, bf16[512,512]{1,0:T(8,128)(2,1)S(1)}, u32[]{:S(2)}, u32[]{:S(2)}) collective-permute-start(bf16[512,512]{1,0:T(8,128)(2,1)S(1)} %get-tuple-element.24.refs_0_), channel_id=1, source_target_pairs={{0,2},{2,4},{4,6},{6,0},{1,3},{3,5},{5,7},{7,1},{8,10},{10,12},{12... | collective-permute-start | bytes 1572872 | tf_op jit(solution)/shard_map/ppermute | solution.py:270
  45.4 20.3 %collective-permute-start.5 = (bf16[512,512]{1,0:T(8,128)(2,1)S(1)}, bf16[512,512]{1,0:T(8,128)(2,1)S(1)}, u32[]{:S(2)}, u32[]{:S(2)}) collective-permute-start(bf16[512,512]{1,0:T(8,128)(2,1)S(1)} %collective-permute-done.1.refs_1_), channel_id=1, source_target_pairs={{0,6},{2,0},{4,2},{6,4},{1,7},{3,1},{5,3},{7,5},{8,14},{10,8},{12,... | collective-permute-start | bytes 1572872 | tf_op jit(solution)/shard_map/ppermute | solution.py:273
  54.4 35.3 %collective-permute-start = (bf16[4096,128]{1,0:T(8,128)(2,1)}, bf16[4096,128]{1,0:T(8,128)(2,1)}, u32[]{:S(2)}, u32[]{:S(2)}) collective-permute-start(bf16[4096,128]{1,0:T(8,128)(2,1)} %bitcast.4.mine), channel_id=1, source_target_pairs={{0,1},{1,0},{2,3},{3,2},{4,5},{5,4},{6,7},{7,6},{8,9},{9,8},{10,11... | collective-permute-start | bytes 3145736 | tf_op jit(solution)/shard_map/ppermute | solution.py:280
  56.3 17.2 %collective-permute-start.3 = (bf16[512,512]{1,0:T(8,128)(2,1)S(1)}, bf16[512,512]{1,0:T(8,128)(2,1)S(1)}, u32[]{:S(2)}, u32[]{:S(2)}) collective-permute-start(bf16[512,512]{1,0:T(8,128)(2,1)S(1)} %get-tuple-element.24.refs_0_), channel_id=1, source_target_pairs={{0,6},{2,0},{4,2},{6,4},{1,7},{3,1},{5,3},{7,5},{8,14},{10,8},{12,... | collective-permute-start | bytes 1572872 | tf_op jit(solution)/shard_map/ppermute | solution.py:271
  61.3 28.5 %collective-permute-start.4 = (bf16[512,512]{1,0:T(8,128)(2,1)S(1)}, bf16[512,512]{1,0:T(8,128)(2,1)S(1)}, u32[]{:S(2)}, u32[]{:S(2)}) collective-permute-start(bf16[512,512]{1,0:T(8,128)(2,1)S(1)} %collective-permute-done.1.refs_1_), channel_id=1, source_target_pairs={{0,2},{2,4},{4,6},{6,0},{1,3},{3,5},{5,7},{7,1},{8,10},{10,12},{12... | collective-permute-start | bytes 1572872 | tf_op jit(solution)/shard_map/ppermute | solution.py:274
  63.2 26.6 %collective-permute-start.6 = (bf16[512,512]{1,0:T(8,128)(2,1)S(1)}, bf16[512,512]{1,0:T(8,128)(2,1)}, u32[]{:S(2)}, u32[]{:S(2)}) collective-permute-start(bf16[512,512]{1,0:T(8,128)(2,1)S(1)} %collective-permute-done.2.refs_2_), channel_id=1, source_target_pairs={{0,2},{2,4},{4,6},{6,0},{1,3},{3,5},{5,7},{7,1},{8,10},{10,12},{12... | collective-permute-start | bytes 1572872 | tf_op jit(solution)/shard_map/ppermute | solution.py:275
  65.7 24.1 %collective-permute-start.7 = (bf16[512,512]{1,0:T(8,128)(2,1)S(1)}, bf16[512,512]{1,0:T(8,128)(2,1)}, u32[]{:S(2)}, u32[]{:S(2)}) collective-permute-start(bf16[512,512]{1,0:T(8,128)(2,1)S(1)} %collective-permute-done.5.refs_5_), channel_id=1, source_target_pairs={{0,6},{2,0},{4,2},{6,4},{1,7},{3,1},{5,3},{7,5},{8,14},{10,8},{12,... | collective-permute-start | bytes 1572872 | tf_op jit(solution)/shard_map/ppermute | solution.py:276
  70.3 0.7 copy-start.10
  70.3 0.7 copy-start.11
  94.0 0.8 copy-start.4
  95.5 3.5 %copy-start.7 = (s32[384]{0:T(512)S(1)}, s32[384]{0:T(512)}, u32[]{:S(2)}) copy-start(s32[384]{0:T(512)} %param.12) | copy-start | bytes 4612
  95.5 9.5 %all-to-all-start.2 = ((bf16[8,16,512]{2,1,0:T(8,128)(2,1)}), bf16[8,16,512]{2,1,0:T(8,128)(2,1)S(1)}, u32[]{:S(2)}, u32[]{:S(2)}) async-start(bf16[8,16,512]{2,1,0:T(8,128)(2,1)} %broadcast_in_dim.30), calls=%async_computation.2 | async-start | bytes 262144 | tf_op jit(solution)/shard_map/all_to_all | solution.py:25
  99.0 0.7 copy-start.8
  105.0 1.0 copy-start
  108.1 8.3 %copy-start.9 = (f32[384]{0:T(512)S(1)}, f32[384]{0:T(512)}, u32[]{:S(2)}) copy-start(f32[384]{0:T(512)} %param.15) | copy-start | bytes 4612
  108.1 22.9 %all-to-all-start.3 = ((f32[64,1,384]{2,1,0:T(1,128)}), f32[64,1,384]{2,1,0:T(1,128)S(1)}, u32[]{:S(2)}, u32[]{:S(2)}) async-start(f32[64,1,384]{2,1,0:T(1,128)} %get-tuple-element.15), calls=%async_computation.3 | async-start | bytes 196608 | tf_op jit(solution)/shard_map/all_to_all | solution.py:304
  131.0 1.0 copy-start.1
  133.0 10.7 %copy-start.5 = (f32[256,512]{1,0:T(8,128)S(1)}, f32[256,512]{1,0:T(8,128)}, u32[]{:S(2)}) copy-start(f32[256,512]{1,0:T(8,128)} %copy-done.4) | copy-start | bytes 1572868
  147.0 8.4 %collective-permute-start.8 = (bf16[2048,128]{1,0:T(8,128)(2,1)S(1)}, bf16[2048,128]{1,0:T(8,128)(2,1)S(1)}, u32[]{:S(2)}, u32[]{:S(2)}) collective-permute-start(bf16[2048,128]{1,0:T(8,128)(2,1)S(1)} %get-tuple-element.18), channel_id=1, source_target_pairs={{0,1},{1,0},{2,3},{3,2},{4,5},{5,4},{6,7},{7,6},{8,9},{9,8},{10,11... | collective-permute-start | bytes 1572872 | tf_op jit(solution)/shard_map/ppermute | solution.py:324
  153.1 3.4 %copy-start.2 = (bf16[2048,128]{1,0:T(8,128)(2,1)}, bf16[2048,128]{1,0:T(8,128)(2,1)S(1)}, u32[]{:S(2)}) copy-start(bf16[2048,128]{1,0:T(8,128)(2,1)S(1)} %get-tuple-element.20) | copy-start | bytes 1572868
  153.1 7.0 %collective-permute-start.9 = (bf16[2048,128]{1,0:T(8,128)(2,1)}, bf16[2048,128]{1,0:T(8,128)(2,1)S(1)}, u32[]{:S(2)}, u32[]{:S(2)}) collective-permute-start(bf16[2048,128]{1,0:T(8,128)(2,1)} %get-tuple-element.21), channel_id=1, source_target_pairs={{0,1},{1,0},{2,3},{3,2},{4,5},{5,4},{6,7},{7,6},{8,9},{9,8},{10,11... | collective-permute-start | bytes 1572872 | tf_op jit(solution)/shard_map/ppermute | solution.py:324
  156.5 3.6 %copy-start.3 = (bf16[2048,128]{1,0:T(8,128)(2,1)S(1)}, bf16[2048,128]{1,0:T(8,128)(2,1)}, u32[]{:S(2)}) copy-start(bf16[2048,128]{1,0:T(8,128)(2,1)} %copy-done.2) | copy-start | bytes 1572868
  156.5 13.5 %all-to-all-start.5 = ((bf16[4,512,128]{2,1,0:T(8,128)(2,1)}), bf16[4,512,128]{2,1,0:T(8,128)(2,1)S(1)}, u32[]{:S(2)}, u32[]{:S(2)}) async-start(bf16[4,512,128]{2,1,0:T(8,128)(2,1)} %bitcast.13), calls=%async_computation.5 | async-start | bytes 1048576 | tf_op jit(solution)/shard_map/all_to_all | solution.py:330
  170.0 12.5 %all-to-all-start.7 = ((bf16[4,512,128]{2,1,0:T(8,128)(2,1)}), bf16[4,512,128]{2,1,0:T(8,128)(2,1)S(1)}, u32[]{:S(2)}, u32[]{:S(2)}) async-start(bf16[4,512,128]{2,1,0:T(8,128)(2,1)} %bitcast.15), calls=%async_computation.7 | async-start | bytes 1048576 | tf_op jit(solution)/shard_map/all_to_all | solution.py:330
  182.5 17.0 %all-to-all-start.6 = ((bf16[16,32,128]{2,1,0:T(8,128)(2,1)}), bf16[16,32,128]{2,1,0:T(8,128)(2,1)S(1)}, u32[]{:S(2)}, u32[]{:S(2)}) async-start(bf16[16,32,128]{2,1,0:T(8,128)(2,1)} %bitcast.14), calls=%async_computation.6 | async-start | bytes 262144 | tf_op jit(solution)/shard_map/all_to_all | solution.py:332
  199.5 17.2 %all-to-all-start.8 = ((bf16[16,32,128]{2,1,0:T(8,128)(2,1)}), bf16[16,32,128]{2,1,0:T(8,128)(2,1)S(1)}, u32[]{:S(2)}, u32[]{:S(2)}) async-start(bf16[16,32,128]{2,1,0:T(8,128)(2,1)} %bitcast.16), calls=%async_computation.8 | async-start | bytes 262144 | tf_op jit(solution)/shard_map/all_to_all | solution.py:332

commit v2 on v0

--- a/solution.py
+++ b/solution.py
@@ -35,7 +35,7 @@
 
 
 def forward_kernel(nb, place, mine, theirs, *refs):
-    blocks, (pooled, slope, feats, held, total, sems) = refs[:nb], refs[nb:]
+    blocks, (pooled, total, feats, held, sems) = refs[:nb], refs[nb:]
     rows = held.shape[1]
     tok = mine.shape[1]
     copies = [
@@ -55,10 +55,7 @@
             total[...] += term
         else:
             total[...] = term
-    logits = total[...]
-    positive = jnp.maximum(logits, 0.0)
-    slope[...] = jnp.where(logits > 0, 1.0 / (1.0 + positive), 0.0)
-    sums = jnp.log1p(positive).reshape(-1, QLEN, logits.shape[1]).sum(1)
+    sums = jnp.log1p(jnp.maximum(total[...], 0.0)).reshape(-1, QLEN, total.shape[1]).sum(1)
     half = sums.shape[0] // 2
     first, second = sums[:half], sums[half:]
     swapped = place[nb] == 1
@@ -82,7 +79,6 @@
         scratch_shapes=[
             pltpu.VMEM((depth, 2 * tok), BF16),
             pltpu.VMEM((nb, rows, cols), BF16),
-            pltpu.VMEM((2 * tok, cols), F32),
             pltpu.SemaphoreType.DMA((nb + 2,)),
         ],
         cost_estimate=pl.CostEstimate(
@@ -94,33 +90,99 @@
     )(place, mine, theirs, *blocks)
 
 
-def backward_kernel(nb, place, grad, slope, *refs):
-    blocks, (out, held, sems) = refs[:nb], refs[nb:]
-    rows = held.shape[1]
-    copies = [pltpu.make_async_copy(blocks[k], held.at[k], sems.at[k]) for k in range(nb)]
+def terms_kernel(
+    pair_count, partials, teacher, pair_query, pair_passage, stored, out, passages, sem
+):
+    copy = pltpu.make_async_copy(stored, passages, sem)
+    copy.start()
+    groups, queries, width = out.shape
+    half = width - LANES
+    cores = passages.shape[1] // half
+    slots = pair_query.shape[1]
+    inv_root = 1.0 / math.sqrt(VOCAB)
+    total = partials[...].sum(0)
+    lines = slots // LANES
+    scores = jnp.concatenate([total[i : i + 1] for i in range(lines)], axis=1) * inv_root
+    is_live = lax.broadcasted_iota(jnp.int32, (1, slots), 1) < pair_count[0]
+    residual = jnp.where(is_live, scores - teacher[...], 0.0)
+    error = jnp.sum(residual * residual)
+    pair_grad = 2.0 * residual * inv_root
+    n_query, n_passage = queries * groups // cores, passages.shape[0]
+    query_hot = pair_query[...] == lax.broadcasted_iota(jnp.int32, (n_query, slots), 0)
+    passage_hot = pair_passage[...] == lax.broadcasted_iota(jnp.int32, (n_passage, slots), 0)
+    table = lax.dot_general(
+        query_hot.astype(F32),
+        jnp.where(passage_hot, pair_grad, 0.0),
+        (((1,), (1,)), ((), ())),
+        precision=lax.Precision.HIGHEST,
+        preferred_element_type=F32,
+    )
+    high = table.astype(BF16)
+    low = (table - high.astype(F32)).astype(BF16)
+    parts = jnp.concatenate([high, low], axis=0)
+    copy.wait()
+    for i in range(cores):
+        both = dot(parts, passages[:, i * half : (i + 1) * half], 1, 0)
+        terms = both[:n_query] + both[n_query:]
+        for k in range(groups // cores):
+            out[k * cores + i, :, :half] = terms[k * queries : (k + 1) * queries]
+    out[:, :, half:] = jnp.full((groups, queries, LANES), error, F32)
+
+
+def query_terms(pair_count, partials, teacher, pair_query, pair_passage, passages, shape):
+    return pl.pallas_call(
+        terms_kernel,
+        name="query_terms",
+        out_shape=jax.ShapeDtypeStruct(shape, F32),
+        in_specs=[SMEM] + [WHOLE] * 4 + [ANY],
+        out_specs=WHOLE,
+        scratch_shapes=[pltpu.VMEM(passages.shape, BF16), pltpu.SemaphoreType.DMA(())],
+        compiler_params=pltpu.CompilerParams(vmem_limit_bytes=16 << 20),
+    )(pair_count, partials, teacher, pair_query, pair_passage, passages)
+
+
+def backward_kernel(nb, place, terms, slope, *refs):
+    blocks, (mine, theirs, loss, held, sems) = refs[:nb], refs[nb:]
+    rows = blocks[0].shape[0]
+    tok, cols = slope.shape
+    copies = []
+    for k in range(nb):
+        start = pl.multiple_of(place[k], rows)
+        copies.append(pltpu.make_async_copy(blocks[k], held.at[pl.ds(start, rows)], sems.at[k]))
+        copies[k].start()
+    total = terms[...].sum(0)
+    loss[...] = total[:1, cols:]
+    half = total.shape[0] // 2
+    swapped = place[nb] == 1
+    one, two = total[:half, :cols], total[half:, :cols]
+    kept = jnp.concatenate([jnp.where(swapped, two, one), jnp.where(swapped, one, two)], axis=0)
+    wide = jnp.broadcast_to(kept[:, None, :], (tok // QLEN, QLEN, cols)).reshape(tok, cols)
+    logit_grad = (wide * slope[...]).astype(BF16)
     for copy in copies:
-        copy.start()
-    tok, cols = slope.shape
-    spread_grad = jnp.broadcast_to(grad[...][:, None, :], (tok // QLEN, QLEN, cols))
-    logit_grad = (spread_grad.reshape(tok, cols) * slope[...]).astype(BF16)
-    for k in range(nb):
-        copies[k].wait()
-        start = pl.multiple_of(place[k], rows)
-        out[pl.ds(start, rows), :] = dot(held[k], logit_grad, 1, 1).astype(BF16)
-
-
-def backward(place, grad, slope, blocks):
+        copy.wait()
+    step = 2 * rows
+    for start in range(0, nb * rows, step):
+        term = dot(held[start : start + step, :], logit_grad, 1, 1).astype(BF16)
+        mine[start : start + step, :] = term[:, : tok // 2]
+        theirs[start : start + step, :] = term[:, tok // 2 :]
+
+
+def backward(place, terms, slope, blocks):
     nb, (rows, cols) = len(blocks), blocks[0].shape
     tok = slope.shape[0]
     depth = nb * rows
     return pl.pallas_call(
         functools.partial(backward_kernel, nb),
         name="backward",
-        out_shape=jax.ShapeDtypeStruct((depth, tok), BF16),
+        out_shape=(
+            jax.ShapeDtypeStruct((depth, tok // 2), BF16),
+            jax.ShapeDtypeStruct((depth, tok // 2), BF16),
+            jax.ShapeDtypeStruct((1, LANES), F32),
+        ),
         in_specs=[SMEM, WHOLE, WHOLE] + [ANY] * nb,
-        out_specs=WHOLE,
+        out_specs=(WHOLE,) * 3,
         scratch_shapes=[
-            pltpu.VMEM((nb, rows, cols), BF16),
+            pltpu.VMEM((depth, cols), BF16),
             pltpu.SemaphoreType.DMA((nb,)),
         ],
         cost_estimate=pl.CostEstimate(
@@ -129,7 +191,7 @@
             transcendentals=0,
         ),
         compiler_params=pltpu.CompilerParams(vmem_limit_bytes=32 << 20),
-    )(place, grad, slope, *blocks)
+    )(place, terms, slope, *blocks)
 
 
 def step(hidden, head, passages, pair_query, pair_passage, pair_count, teacher):
@@ -172,61 +234,42 @@
     steps = jnp.array([step for step, _, _ in held], jnp.int32)
     others = jnp.array([other for _, other, _ in held], jnp.int32)
     owner = ((y + steps) % ny) * nc + (c + others) % nc
-    place = jnp.concatenate([owner * rows, c[None]]).astype(jnp.int32)
-
-    both, slope = forward(place, mine, theirs, blocks)
+    place = jnp.concatenate([owner * rows, c[None], y[None]]).astype(jnp.int32)
+
+    both, logits = forward(place, mine, theirs, blocks)
     every = spread(both, ("y", "c"), batch).reshape(ny, nc, nc * queries, half)
     halves = [every[:, i].reshape(batch * queries, half) for i in range(nc)]
     wide = jnp.concatenate(halves, axis=1)
     pooled = lax.dynamic_slice_in_dim(wide, (y * nc + c) * queries, queries, 0)
 
-    inv_root = 1.0 / math.sqrt(VOCAB)
     slots = pair_query.shape[0]
     n_query, n_passage = batch * queries, passages.shape[0]
+    pair_query, pair_passage = pair_query.reshape(1, slots), pair_passage.reshape(1, slots)
     table = dot(passages, wide, 1, 1)
-    query_hot = (pair_query[None, :] == jnp.arange(n_query, dtype=jnp.int32)[:, None]).astype(F32)
-    passage_hot = (
-        pair_passage[None, :] == jnp.arange(n_passage, dtype=jnp.int32)[:, None]
-    ).astype(F32)
+    query_hot = (pair_query == jnp.arange(n_query, dtype=jnp.int32)[:, None]).astype(F32)
+    passage_hot = (pair_passage == jnp.arange(n_passage, dtype=jnp.int32)[:, None]).astype(F32)
     spread_table = jnp.dot(table, query_hot, precision=lax.Precision.HIGHEST)
     partial_value = (spread_table * passage_hot).sum(0)
     packed = jnp.pad(partial_value, (0, -slots % 512)).reshape(-1, LANES)
-    packed = spread(packed, ("x", "z"), nx * nz).sum(0)
-    scores = packed.reshape(-1)[:slots] * inv_root
-
-    is_live = jnp.arange(slots, dtype=jnp.int32) < pair_count[0]
-    residual = jnp.where(is_live, scores - teacher, 0.0)
-    error = jnp.sum(residual * residual)
-    pair_grad = 2.0 * residual * inv_root
-    pair_table = lax.dot_general(
-        query_hot,
-        passage_hot * pair_grad[None, :],
-        (((1,), (1,)), ((), ())),
-        precision=lax.Precision.HIGHEST,
+    partials = spread(packed, ("x", "z"), nx * nz)
+    positive = jnp.maximum(logits, 0.0)
+    slope = jnp.where(logits > 0, 1.0 / (1.0 + positive), 0.0)
+
+    terms = query_terms(
+        pair_count,
+        partials,
+        teacher.reshape(1, slots),
+        pair_query,
+        pair_passage,
+        passages,
+        (batch, nc * queries, half + LANES),
     )
-    table_high = pair_table.astype(BF16)
-    table_low = (pair_table - table_high.astype(F32)).astype(BF16)
-    query_terms = dot(table_high, passages, 1, 0) + dot(table_low, passages, 1, 0)
-    terms = jnp.stack(
-        [
-            query_terms[:, i * half : (i + 1) * half].reshape(ny, nc * queries, half)
-            for i in range(nc)
-        ],
-        axis=1,
-    ).reshape(batch, nc * queries, half)
-    terms = jnp.concatenate(
-        [terms, jnp.broadcast_to(error, (batch, nc * queries, LANES))], axis=2
-    )
-    terms = lax.all_to_all(terms, ("y", "c"), 0, 0, tiled=True).sum(0)
-    loss_value = terms[0, half] / (slots * batch)
-    grads = terms[:, :half].reshape(nc, queries, half)
-    grad_mine = lax.dynamic_index_in_dim(grads, c, 0, keepdims=False)
-    grad_theirs = lax.dynamic_index_in_dim(grads, 1 - c, 0, keepdims=False)
-
-    terms_theirs = backward(place, grad_theirs, slope[tok:], blocks)
-    terms_pair = lax.ppermute(terms_theirs, "c", swap)
-    terms_mine = backward(place, grad_mine, slope[:tok], blocks)
-    hidden_terms = (terms_mine.astype(F32) + terms_pair.astype(F32)).astype(BF16)
+    terms = lax.all_to_all(terms, ("y", "c"), 0, 0, tiled=True)
+
+    kept, sent, loss = backward(place, terms, slope, blocks)
+    loss_value = loss[0, 0] / (slots * batch)
+    other = lax.ppermute(sent, "c", swap)
+    hidden_terms = (kept.astype(F32) + other.astype(F32)).astype(BF16)
     hidden_terms = hidden_terms.reshape(nx, nz * feat, tok)
     over_x = lax.all_to_all(hidden_terms, "x", 0, 0, tiled=True)
     over_x = over_x.astype(F32).sum(0).astype(BF16).reshape(nz, feat, tok)

time: 203 us -> 194 us (0.956)
  the two profiles are of different devices: /device:TPU:32 before, /device:TPU:64 now
where the time goes in v2:
time: 194 us; the launch traced here: 193 us
  waiting for transfers between devices  63.6 us (33%)
  blocking collectives  59.6 us (31%)
  starting transfers between devices  50.1 us (26%)
  Pallas kernels  9.43 us (5%)
  other arithmetic  3.65 us (2%)
  local copies, waits for them, and re-layouts  3.51 us (2%)
  between operations  2.74 us (1%)
    all_to_all x2, blocking collectives, spread(): lax.all_to_all(jnp.broadcast_to(value[None], (n,) + value.shape), axes, 0...  41.2 us
    all_to_all x1, blocking collectives, step(): over_x = lax.all_to_all(hidden_terms, 'x', 0, 0, tiled=True)  18.4 us
    all_to_all x1, waiting for transfers between devices, step(): over_z = lax.all_to_all(over_x, 'z', 0, 0, tiled=True)  17.4 us
    all_to_all x2, waiting for transfers between devices, spread(): lax.all_to_all(jnp.broadcast_to(value[None], (n,) + value.shape), axes, 0...  17.2 us
    all_to_all x2, starting transfers between devices, spread(): lax.all_to_all(jnp.broadcast_to(value[None], (n,) + value.shape), axes, 0...  14.8 us
    ppermute x1, waiting for transfers between devices, step(): far_own = lax.ppermute(prev_own, 'y', plus)  10.5 us
    all_to_all x1, waiting for transfers between devices, step(): terms = lax.all_to_all(terms, ('y', 'c'), 0, 0, tiled=True)  7 us
    ppermute x1, waiting for transfers between devices, step(): next_own = lax.ppermute(own, 'y', minus)  5.74 us
  transfers between devices with their start and end apart: 13, of which 8 were waited for; matrix products, arithmetic and copies ran while one was open for 1% of the time, Pallas kernels for 0%

profile of v2, /device:TPU:64, one launch (start us, length us, event | category | flops | bytes accessed | tf_op | source)
XLA Modules:
  0.0 193.3 jit_solution(18291818772862126903)
XLA Ops:
  0.6 0.8 broadcast_in_dim.38
  1.4 32.6 %all_to_all.35 = bf16[16,64,128]{2,1,0:T(8,128)(2,1)S(1)} all-to-all(bf16[16,64,128]{2,1,0:T(8,128)(2,1)S(1)} %broadcast_in_dim.38), channel_id=1, replica_groups=mesh['x'=4,'z'=16,'y'=4,'c'=2] {'z'}, dimensions={0} | all-to-all | bytes 524288 | tf_op jit(solution)/shard_map/all_to_all | solution.py:25
  34.0 1.1 broadcast_in_dim.40
  35.1 4.4 %all-to-all-start.1 = ((bf16[4,1024,128]{2,1,0:T(8,128)(2,1)}), bf16[4,1024,128]{2,1,0:T(8,128)(2,1)S(1)}, u32[]{:S(2)}, u32[]{:S(2)}) async-start(bf16[4,1024,128]{2,1,0:T(8,128)(2,1)} %broadcast_in_dim.40), calls=%async_computation.1 | async-start | bytes 2097152 | tf_op jit(solution)/shard_map/all_to_all | solution.py:25
  39.6 0.0 copy-done.2
  39.6 0.1 constant_dynamic-slice_fusion
  39.7 1.9 collective-permute-start.1
  41.6 3.5 %collective-permute-start.2 = (bf16[512,512]{1,0:T(8,128)(2,1)S(1)}, bf16[512,512]{1,0:T(8,128)(2,1)S(1)}, u32[]{:S(2)}, u32[]{:S(2)}) collective-permute-start(bf16[512,512]{1,0:T(8,128)(2,1)S(1)} %get-tuple-element.14.refs_0_), channel_id=1, source_target_pairs={{0,2},{2,4},{4,6},{6,0},{1,3},{3,5},{5,7},{7,1},{8,10},{10,12},{12... | collective-permute-start | bytes 1572872 | tf_op jit(solution)/shard_map/ppermute | solution.py:211
  45.1 0.0 collective-permute-done.1.refs_1_
  45.1 3.6 %collective-permute-start.5 = (bf16[512,512]{1,0:T(8,128)(2,1)S(1)}, bf16[512,512]{1,0:T(8,128)(2,1)}, u32[]{:S(2)}, u32[]{:S(2)}) collective-permute-start(bf16[512,512]{1,0:T(8,128)(2,1)S(1)} %collective-permute-done.1.refs_1_), channel_id=1, source_target_pairs={{0,6},{2,0},{4,2},{6,4},{1,7},{3,1},{5,3},{7,5},{8,14},{10,8},{12,... | collective-permute-start | bytes 1572872 | tf_op jit(solution)/shard_map/ppermute | solution.py:214
  48.7 2.7 %all-to-all-done.1 = bf16[4,1024,128]{2,1,0:T(8,128)(2,1)S(1)} async-done(((bf16[4,1024,128]{2,1,0:T(8,128)(2,1)}), bf16[4,1024,128]{2,1,0:T(8,128)(2,1)S(1)}, u32[]{:S(2)}, u32[]{:S(2)}) %all-to-all-start.1) | async-done | bytes 1048608 | tf_op jit(solution)/shard_map/all_to_all | solution.py:25
  51.4 1.9 collective-permute-start
  53.3 4.9 %collective-permute-start.3 = (bf16[512,512]{1,0:T(8,128)(2,1)S(1)}, bf16[512,512]{1,0:T(8,128)(2,1)}, u32[]{:S(2)}, u32[]{:S(2)}) collective-permute-start(bf16[512,512]{1,0:T(8,128)(2,1)S(1)} %get-tuple-element.14.refs_0_), channel_id=1, source_target_pairs={{0,6},{2,0},{4,2},{6,4},{1,7},{3,1},{5,3},{7,5},{8,14},{10,8},{12,... | collective-permute-start | bytes 1572872 | tf_op jit(solution)/shard_map/ppermute | solution.py:212
  58.3 1.9 collective-permute-start.4
  60.2 0.0 collective-permute-done.2.refs_2_
  60.2 2.5 %collective-permute-start.6 = (bf16[512,512]{1,0:T(8,128)(2,1)S(1)}, bf16[512,512]{1,0:T(8,128)(2,1)}, u32[]{:S(2)}, u32[]{:S(2)}) collective-permute-start(bf16[512,512]{1,0:T(8,128)(2,1)S(1)} %collective-permute-done.2.refs_2_), channel_id=1, source_target_pairs={{0,2},{2,4},{4,6},{6,0},{1,3},{3,5},{5,7},{7,1},{8,10},{10,12},{12... | collective-permute-start | bytes 1572872 | tf_op jit(solution)/shard_map/ppermute | solution.py:216
  62.7 0.0 collective-permute-done.5.refs_5_
  62.7 4.6 %collective-permute-start.7 = (bf16[512,512]{1,0:T(8,128)(2,1)}, bf16[512,512]{1,0:T(8,128)(2,1)}, u32[]{:S(2)}, u32[]{:S(2)}) collective-permute-start(bf16[512,512]{1,0:T(8,128)(2,1)} %collective-permute-done.5.refs_5_), channel_id=1, source_target_pairs={{0,6},{2,0},{4,2},{6,4},{1,7},{3,1},{5,3},{7,5},{8,14},{10,8},{12,... | collective-permute-start | bytes 1572872 | tf_op jit(solution)/shard_map/ppermute | solution.py:217
  67.3 0.1 pad_add_fusion.place
  67.4 5.7 %collective-permute-done.3.refs_3_ = bf16[512,512]{1,0:T(8,128)(2,1)} collective-permute-done((bf16[512,512]{1,0:T(8,128)(2,1)S(1)}, bf16[512,512]{1,0:T(8,128)(2,1)}, u32[]{:S(2)}, u32[]{:S(2)}) %collective-permute-start.3) | collective-permute-done | bytes 524320 | tf_op jit(solution)/shard_map/ppermute | solution.py:212
  73.2 3.1 %collective-permute-done.4.refs_4_ = bf16[512,512]{1,0:T(8,128)(2,1)} collective-permute-done((bf16[512,512]{1,0:T(8,128)(2,1)S(1)}, bf16[512,512]{1,0:T(8,128)(2,1)}, u32[]{:S(2)}, u32[]{:S(2)}) %collective-permute-start.4) | collective-permute-done | bytes 524320 | tf_op jit(solution)/shard_map/ppermute | solution.py:215
  76.3 10.5 %collective-permute-done.6.refs_6_ = bf16[512,512]{1,0:T(8,128)(2,1)} collective-permute-done((bf16[512,512]{1,0:T(8,128)(2,1)S(1)}, bf16[512,512]{1,0:T(8,128)(2,1)}, u32[]{:S(2)}, u32[]{:S(2)}) %collective-permute-start.6) | collective-permute-done | bytes 524320 | tf_op jit(solution)/shard_map/ppermute | solution.py:216
  86.8 0.0 collective-permute-done.7.refs_7_
  86.8 0.0 collective-permute-done.theirs
  86.8 4.1 %forward.1 = (bf16[16,512]{1,0:T(8,128)(2,1)S(1)}, f32[256,512]{1,0:T(8,128)S(1)}) custom-call(s32[10]{0:T(128)S(1)} %pad_add_fusion.place, bf16[4096,128]{1,0:T(8,128)(2,1)S(1)} %bitcast.18, bf16[4096,128]{1,0:T(8,128)(2,1)} %collective-permute-done.theirs, bf16[512,512]{1,0:T(8,128)(2,1)S(1)} %get-tuple-element.14.refs_0_, ...), custom_call_target="tpu_custom_call" | custom-call | flops 1073741824 | bytes 6815744 | tf_op jit(solution)/shard_map/forward/pallas_call | solution.py:70
  90.8 0.8 copy-done.1
  91.6 0.0 copy-start.5
  91.7 8.6 %all_to_all.36 = bf16[8,16,512]{2,1,0:T(8,128)(2,1)S(1)} all-to-all(bf16[8,16,512]{2,1,0:T(8,128)(2,1)S(1)} %broadcast_in_dim.41), channel_id=1, replica_groups=mesh['x'=4,'z'=16,'y'=4,'c'=2] {'y','c'}, dimensions={0} | all-to-all | bytes 262144 | tf_op jit(solution)/shard_map/all_to_all | solution.py:25
  100.3 0.0 copy-done
  100.3 0.3 fusion.1
  100.6 0.4 fusion
  101.0 0.7 broadcast_in_dim.43
  101.7 10.4 %all-to-all-start.3 = ((f32[64,4,128]{2,1,0:T(4,128)}), f32[64,4,128]{2,1,0:T(4,128)S(1)}, u32[]{:S(2)}, u32[]{:S(2)}) async-start(f32[64,4,128]{2,1,0:T(4,128)} %broadcast_in_dim.43), calls=%async_computation.3 | async-start | bytes 262144 | tf_op jit(solution)/shard_map/all_to_all | solution.py:25
  112.8 14.4 %all-to-all-done.3.partials = f32[64,4,128]{2,1,0:T(4,128)S(1)} async-done(((f32[64,4,128]{2,1,0:T(4,128)}), f32[64,4,128]{2,1,0:T(4,128)S(1)}, u32[]{:S(2)}, u32[]{:S(2)}) %all-to-all-start.3) | async-done | bytes 131104 | tf_op jit(solution)/shard_map/all_to_all | solution.py:25
  127.2 1.7 query_terms.1
  128.9 3.4 %all-to-all-start.4 = ((f32[8,16,640]{2,1,0:T(8,128)}), f32[8,16,640]{2,1,0:T(8,128)S(1)}, u32[]{:S(2)}, u32[]{:S(2)}) async-start(f32[8,16,640]{2,1,0:T(8,128)} %query_terms.1), calls=%async_computation.4 | async-start | bytes 655360 | tf_op jit(solution)/shard_map/all_to_all | solution.py:267
  132.4 1.1 divide_select_fusion.slope
  133.5 7.0 %all-to-all-done.4.terms = f32[8,16,640]{2,1,0:T(8,128)S(1)} async-done(((f32[8,16,640]{2,1,0:T(8,128)}), f32[8,16,640]{2,1,0:T(8,128)S(1)}, u32[]{:S(2)}, u32[]{:S(2)}) %all-to-all-start.4) | async-done | bytes 327712 | tf_op jit(solution)/shard_map/all_to_all | solution.py:267
  140.5 3.7 %backward.1 = (bf16[4096,128]{1,0:T(8,128)(2,1)S(1)}, bf16[4096,128]{1,0:T(8,128)(2,1)S(1)}, f32[1,128]{1,0:T(1,128)S(1)}) custom-call(s32[10]{0:T(128)S(1)} %pad_add_fusion.place, f32[8,16,640]{2,1,0:T(8,128)S(1)} %all-to-all-done.4.terms, f32[256,512]{1,0:T(8,128)S(1)} %divide_select_fusion.slope, bf16[512,512]{1,0:T(8,128)(2,1)S(1)} %get-tuple-element.14.refs_0_, ...), custom_call_target="tpu_custom_call" | custom-call | flops 1073741824 | bytes 6815744 | tf_op jit(solution)/shard_map/backward/pallas_call | solution.py:174
  144.2 1.9 collective-permute-start.8
  146.1 2.6 %collective-permute-done.8 = bf16[4096,128]{1,0:T(8,128)(2,1)S(1)} collective-permute-done((bf16[4096,128]{1,0:T(8,128)(2,1)S(1)}, bf16[4096,128]{1,0:T(8,128)(2,1)S(1)}, u32[]{:S(2)}, u32[]{:S(2)}) %collective-permute-start.8) | collective-permute-done | bytes 1048608 | tf_op jit(solution)/shard_map/ppermute | solution.py:271
  148.8 0.3 add_convert_fusion
  149.0 18.4 %all_to_all.37 = bf16[4,1024,128]{2,1,0:T(8,128)(2,1)S(1)} all-to-all(bf16[4,1024,128]{2,1,0:T(8,128)(2,1)S(1)} %bitcast.20), channel_id=1, replica_groups=mesh['x'=4,'z'=16,'y'=4,'c'=2] {'x'}, dimensions={0} | all-to-all | bytes 2097152 | tf_op jit(solution)/shard_map/all_to_all | solution.py:274
  167.4 0.9 reduce_sum.34
  168.3 5.1 %all-to-all-start.6 = ((bf16[16,64,128]{2,1,0:T(8,128)(2,1)}), bf16[16,64,128]{2,1,0:T(8,128)(2,1)S(1)}, u32[]{:S(2)}, u32[]{:S(2)}) async-start(bf16[16,64,128]{2,1,0:T(8,128)(2,1)} %bitcast.10), calls=%async_computation.6 | async-start | bytes 524288 | tf_op jit(solution)/shard_map/all_to_all | solution.py:276
  173.5 0.6 fusion.3
  174.1 17.4 %all-to-all-done.6 = bf16[16,64,128]{2,1,0:T(8,128)(2,1)S(1)} async-done(((bf16[16,64,128]{2,1,0:T(8,128)(2,1)}), bf16[16,64,128]{2,1,0:T(8,128)(2,1)S(1)}, u32[]{:S(2)}, u32[]{:S(2)}) %all-to-all-start.6) | async-done | bytes 262176 | tf_op jit(solution)/shard_map/all_to_all | solution.py:276
  191.5 0.6 reduce_sum.35
  (19 shorter events, 0.1 us)
Async XLA Ops:
  35.1 4.4 %copy-start.2 = (bf16[512,1024]{1,0:T(8,128)(2,1)S(1)}, bf16[512,1024]{1,0:T(8,128)(2,1)}, u32[]{:S(2)}) copy-start(bf16[512,1024]{1,0:T(8,128)(2,1)} %param.10) | copy-start | bytes 3145732
  35.1 16.3 %all-to-all-start.1 = ((bf16[4,1024,128]{2,1,0:T(8,128)(2,1)}), bf16[4,1024,128]{2,1,0:T(8,128)(2,1)S(1)}, u32[]{:S(2)}, u32[]{:S(2)}) async-start(bf16[4,1024,128]{2,1,0:T(8,128)(2,1)} %broadcast_in_dim.40), calls=%async_computation.1 | async-start | bytes 2097152 | tf_op jit(solution)/shard_map/all_to_all | solution.py:25
  39.6 27.7 %copy-start.6 = (s32[8]{0:T(128)S(1)}, s32[8]{0:T(128)}, u32[]{:S(2)}) copy-start(s32[8]{0:T(128)} %constant.65.clone) | copy-start | bytes 100
  39.6 27.7 %copy-start.7 = (s32[8]{0:T(128)S(1)}, s32[8]{0:T(128)}, u32[]{:S(2)}) copy-start(s32[8]{0:T(128)} %constant.64.clone) | copy-start | bytes 100
  39.7 5.4 %collective-permute-start.1 = (bf16[512,512]{1,0:T(8,128)(2,1)S(1)}, bf16[512,512]{1,0:T(8,128)(2,1)S(1)}, u32[]{:S(2)}, u32[]{:S(2)}) collective-permute-start(bf16[512,512]{1,0:T(8,128)(2,1)S(1)} %get-tuple-element.13), channel_id=1, source_target_pairs={{0,1},{1,0},{2,3},{3,2},{4,5},{5,4},{6,7},{7,6},{8,9},{9,8},{10,11... | collective-permute-start | bytes 1572872 | tf_op jit(solution)/shard_map/ppermute | solution.py:213
  41.6 18.6 %collective-permute-start.2 = (bf16[512,512]{1,0:T(8,128)(2,1)S(1)}, bf16[512,512]{1,0:T(8,128)(2,1)S(1)}, u32[]{:S(2)}, u32[]{:S(2)}) collective-permute-start(bf16[512,512]{1,0:T(8,128)(2,1)S(1)} %get-tuple-element.14.refs_0_), channel_id=1, source_target_pairs={{0,2},{2,4},{4,6},{6,0},{1,3},{3,5},{5,7},{7,1},{8,10},{10,12},{12... | collective-permute-start | bytes 1572872 | tf_op jit(solution)/shard_map/ppermute | solution.py:211
  45.1 17.6 %collective-permute-start.5 = (bf16[512,512]{1,0:T(8,128)(2,1)S(1)}, bf16[512,512]{1,0:T(8,128)(2,1)}, u32[]{:S(2)}, u32[]{:S(2)}) collective-permute-start(bf16[512,512]{1,0:T(8,128)(2,1)S(1)} %collective-permute-done.1.refs_1_), channel_id=1, source_target_pairs={{0,6},{2,0},{4,2},{6,4},{1,7},{3,1},{5,3},{7,5},{8,14},{10,8},{12,... | collective-permute-start | bytes 1572872 | tf_op jit(solution)/shard_map/ppermute | solution.py:214
  51.4 35.3 %collective-permute-start = (bf16[4096,128]{1,0:T(8,128)(2,1)S(1)}, bf16[4096,128]{1,0:T(8,128)(2,1)}, u32[]{:S(2)}, u32[]{:S(2)}) collective-permute-start(bf16[4096,128]{1,0:T(8,128)(2,1)S(1)} %bitcast.17), channel_id=1, source_target_pairs={{0,1},{1,0},{2,3},{3,2},{4,5},{5,4},{6,7},{7,6},{8,9},{9,8},{10,11... | collective-permute-start | bytes 3145736 | tf_op jit(solution)/shard_map/ppermute | solution.py:221
  53.3 19.8 %collective-permute-start.3 = (bf16[512,512]{1,0:T(8,128)(2,1)S(1)}, bf16[512,512]{1,0:T(8,128)(2,1)}, u32[]{:S(2)}, u32[]{:S(2)}) collective-permute-start(bf16[512,512]{1,0:T(8,128)(2,1)S(1)} %get-tuple-element.14.refs_0_), channel_id=1, source_target_pairs={{0,6},{2,0},{4,2},{6,4},{1,7},{3,1},{5,3},{7,5},{8,14},{10,8},{12,... | collective-permute-start | bytes 1572872 | tf_op jit(solution)/shard_map/ppermute | solution.py:212
  58.3 18.0 %collective-permute-start.4 = (bf16[512,512]{1,0:T(8,128)(2,1)S(1)}, bf16[512,512]{1,0:T(8,128)(2,1)}, u32[]{:S(2)}, u32[]{:S(2)}) collective-permute-start(bf16[512,512]{1,0:T(8,128)(2,1)S(1)} %collective-permute-done.1.refs_1_), channel_id=1, source_target_pairs={{0,2},{2,4},{4,6},{6,0},{1,3},{3,5},{5,7},{7,1},{8,10},{10,12},{12... | collective-permute-start | bytes 1572872 | tf_op jit(solution)/shard_map/ppermute | solution.py:215
  60.2 26.6 %collective-permute-start.6 = (bf16[512,512]{1,0:T(8,128)(2,1)S(1)}, bf16[512,512]{1,0:T(8,128)(2,1)}, u32[]{:S(2)}, u32[]{:S(2)}) collective-permute-start(bf16[512,512]{1,0:T(8,128)(2,1)S(1)} %collective-permute-done.2.refs_2_), channel_id=1, source_target_pairs={{0,2},{2,4},{4,6},{6,0},{1,3},{3,5},{5,7},{7,1},{8,10},{10,12},{12... | collective-permute-start | bytes 1572872 | tf_op jit(solution)/shard_map/ppermute | solution.py:216
  62.7 24.1 %collective-permute-start.7 = (bf16[512,512]{1,0:T(8,128)(2,1)}, bf16[512,512]{1,0:T(8,128)(2,1)}, u32[]{:S(2)}, u32[]{:S(2)}) collective-permute-start(bf16[512,512]{1,0:T(8,128)(2,1)} %collective-permute-done.5.refs_5_), channel_id=1, source_target_pairs={{0,6},{2,0},{4,2},{6,4},{1,7},{3,1},{5,3},{7,5},{8,14},{10,8},{12,... | collective-permute-start | bytes 1572872 | tf_op jit(solution)/shard_map/ppermute | solution.py:217
  67.4 32.9 %copy-start = (bf16[256,1024]{1,0:T(8,128)(2,1)S(1)}, bf16[256,1024]{1,0:T(8,128)(2,1)}, u32[]{:S(2)}) copy-start(bf16[256,1024]{1,0:T(8,128)(2,1)} %stored.1) | copy-start | bytes 1572868
  90.8 0.8 copy-start.1
  91.6 9.0 %copy-start.3 = (s32[384]{0:T(512)S(1)}, s32[384]{0:T(512)}, u32[]{:S(2)}) copy-start(s32[384]{0:T(512)} %param.12) | copy-start | bytes 4612
  91.6 9.0 %copy-start.4 = (s32[384]{0:T(512)S(1)}, s32[384]{0:T(512)}, u32[]{:S(2)}) copy-start(s32[384]{0:T(512)} %param.13) | copy-start | bytes 4612
  91.6 21.1 %copy-start.5 = (f32[384]{0:T(512)S(1)}, f32[384]{0:T(512)}, u32[]{:S(2)}) copy-start(f32[384]{0:T(512)} %param.15) | copy-start | bytes 4612
  101.7 25.6 %all-to-all-start.3 = ((f32[64,4,128]{2,1,0:T(4,128)}), f32[64,4,128]{2,1,0:T(4,128)S(1)}, u32[]{:S(2)}, u32[]{:S(2)}) async-start(f32[64,4,128]{2,1,0:T(4,128)} %broadcast_in_dim.43), calls=%async_computation.3 | async-start | bytes 262144 | tf_op jit(solution)/shard_map/all_to_all | solution.py:25
  128.9 11.6 %all-to-all-start.4 = ((f32[8,16,640]{2,1,0:T(8,128)}), f32[8,16,640]{2,1,0:T(8,128)S(1)}, u32[]{:S(2)}, u32[]{:S(2)}) async-start(f32[8,16,640]{2,1,0:T(8,128)} %query_terms.1), calls=%async_computation.4 | async-start | bytes 655360 | tf_op jit(solution)/shard_map/all_to_all | solution.py:267
  144.2 4.6 %collective-permute-start.8 = (bf16[4096,128]{1,0:T(8,128)(2,1)S(1)}, bf16[4096,128]{1,0:T(8,128)(2,1)S(1)}, u32[]{:S(2)}, u32[]{:S(2)}) collective-permute-start(bf16[4096,128]{1,0:T(8,128)(2,1)S(1)} %get-tuple-element.11), channel_id=1, source_target_pairs={{0,1},{1,0},{2,3},{3,2},{4,5},{5,4},{6,7},{7,6},{8,9},{9,8},{10,11... | collective-permute-start | bytes 3145736 | tf_op jit(solution)/shard_map/ppermute | solution.py:271
  168.3 23.2 %all-to-all-start.6 = ((bf16[16,64,128]{2,1,0:T(8,128)(2,1)}), bf16[16,64,128]{2,1,0:T(8,128)(2,1)S(1)}, u32[]{:S(2)}, u32[]{:S(2)}) async-start(bf16[16,64,128]{2,1,0:T(8,128)(2,1)} %bitcast.10), calls=%async_computation.6 | async-start | bytes 524288 | tf_op jit(solution)/shard_map/all_to_all | solution.py:276

commit v3 on v2

--- a/solution.py
+++ b/solution.py
@@ -21,6 +21,12 @@
     return [(i, (i + step) % n) for i in range(n)]
 
 
+def cross(ny, nc, step):
+    return [
+        (y * nc + c, ((y + step) % ny) * nc + (c + 1) % nc) for y in range(ny) for c in range(nc)
+    ]
+
+
 def spread(value, axes, n):
     return lax.all_to_all(jnp.broadcast_to(value[None], (n,) + value.shape), axes, 0, 0, tiled=True)
 
@@ -35,7 +41,7 @@
 
 
 def forward_kernel(nb, place, mine, theirs, *refs):
-    blocks, (pooled, total, feats, held, sems) = refs[:nb], refs[nb:]
+    blocks, (pooled, logits, feats, held, total, sems) = refs[:nb], refs[nb:]
     rows = held.shape[1]
     tok = mine.shape[1]
     copies = [
@@ -55,12 +61,15 @@
             total[...] += term
         else:
             total[...] = term
+    keep = pltpu.make_async_copy(total, logits, sems.at[nb + 2])
+    keep.start()
     sums = jnp.log1p(jnp.maximum(total[...], 0.0)).reshape(-1, QLEN, total.shape[1]).sum(1)
     half = sums.shape[0] // 2
     first, second = sums[:half], sums[half:]
     swapped = place[nb] == 1
     pooled[:half, :] = jnp.where(swapped, second, first).astype(BF16)
     pooled[half:, :] = jnp.where(swapped, first, second).astype(BF16)
+    keep.wait()
 
 
 def forward(place, mine, theirs, blocks):
@@ -75,11 +84,12 @@
             jax.ShapeDtypeStruct((2 * tok, cols), F32),
         ),
         in_specs=[SMEM] + [ANY] * (2 + nb),
-        out_specs=(WHOLE, WHOLE),
+        out_specs=(WHOLE, ANY),
         scratch_shapes=[
             pltpu.VMEM((depth, 2 * tok), BF16),
             pltpu.VMEM((nb, rows, cols), BF16),
-            pltpu.SemaphoreType.DMA((nb + 2,)),
+            pltpu.VMEM((2 * tok, cols), F32),
+            pltpu.SemaphoreType.DMA((nb + 3,)),
         ],
         cost_estimate=pl.CostEstimate(
             flops=4 * tok * depth * cols,
@@ -125,15 +135,19 @@
         both = dot(parts, passages[:, i * half : (i + 1) * half], 1, 0)
         terms = both[:n_query] + both[n_query:]
         for k in range(groups // cores):
-            out[k * cores + i, :, :half] = terms[k * queries : (k + 1) * queries]
-    out[:, :, half:] = jnp.full((groups, queries, LANES), error, F32)
+            out[k * cores + i, :, :half] = terms[k * queries : (k + 1) * queries].astype(BF16)
+    errors = jnp.full((groups, queries, LANES), error, F32)
+    error_high = errors.astype(BF16)
+    error_low = (errors - error_high.astype(F32)).astype(BF16)
+    lane = lax.broadcasted_iota(jnp.int32, errors.shape, 2)
+    out[:, :, half:] = jnp.where(lane < LANES // 2, error_high, error_low)
 
 
 def query_terms(pair_count, partials, teacher, pair_query, pair_passage, passages, shape):
     return pl.pallas_call(
         terms_kernel,
         name="query_terms",
-        out_shape=jax.ShapeDtypeStruct(shape, F32),
+        out_shape=jax.ShapeDtypeStruct(shape, BF16),
         in_specs=[SMEM] + [WHOLE] * 4 + [ANY],
         out_specs=WHOLE,
         scratch_shapes=[pltpu.VMEM(passages.shape, BF16), pltpu.SemaphoreType.DMA(())],
@@ -150,7 +164,7 @@
         start = pl.multiple_of(place[k], rows)
         copies.append(pltpu.make_async_copy(blocks[k], held.at[pl.ds(start, rows)], sems.at[k]))
         copies[k].start()
-    total = terms[...].sum(0)
+    total = terms[...].astype(F32).sum(0)
     loss[...] = total[:1, cols:]
     half = total.shape[0] // 2
     swapped = place[nb] == 1
@@ -208,13 +222,14 @@
 
     own = lax.dynamic_slice_in_dim(head, c * half, half, 1)
     sent = lax.dynamic_slice_in_dim(head, (1 - c) * half, half, 1)
+    cross_plus, cross_minus = cross(ny, nc, 1), cross(ny, nc, ny - 1)
+    next_pair = lax.ppermute(sent, ("y", "c"), cross_minus)
     prev_own = lax.ppermute(own, "y", plus)
     next_own = lax.ppermute(own, "y", minus)
-    pair = lax.ppermute(sent, "c", swap)
-    next_pair = lax.ppermute(pair, "y", minus)
-    prev_pair = lax.ppermute(pair, "y", plus)
+    prev_pair = lax.ppermute(sent, ("y", "c"), cross_plus)
     far_own = lax.ppermute(prev_own, "y", plus)
     far_pair = lax.ppermute(next_pair, "y", minus)
+    pair = lax.ppermute(sent, "c", swap)
 
     part = spread(hidden.T, "z", nz).reshape(nz * feat, tok)
     mine = spread(part, "x", nx).reshape(nx * nz * feat, tok)
@@ -267,7 +282,7 @@
     terms = lax.all_to_all(terms, ("y", "c"), 0, 0, tiled=True)
 
     kept, sent, loss = backward(place, terms, slope, blocks)
-    loss_value = loss[0, 0] / (slots * batch)
+    loss_value = (loss[0, 0] + loss[0, LANES - 1]) / (slots * batch)
     other = lax.ppermute(sent, "c", swap)
     hidden_terms = (kept.astype(F32) + other.astype(F32)).astype(BF16)
     hidden_terms = hidden_terms.reshape(nx, nz * feat, tok)

time: 194 us -> 193 us (level)
    ppermute x1, waiting for transfers between devices: 0.01 us -> 10.2 us  [step(): far_pair = lax.ppermute(next_pair, 'y', minus)]
    ppermute x1, waiting for transfers between devices: 10.5 us -> 2.97 us  [step(): far_own = lax.ppermute(prev_own, 'y', plus)]
    ppermute x1, waiting for transfers between devices: 0.01 us -> 6.91 us  [step(): prev_own = lax.ppermute(own, 'y', plus)]
    ppermute x1, waiting for transfers between devices: 5.74 us -> 0.01 us  [step(): next_own = lax.ppermute(own, 'y', minus)]
    ppermute x2, waiting for transfers between devices: 3.12 us -> 0.89 us  [the longest x1 0.88 us: step(): next_pair = lax.ppermute(sent, ('y', 'c'), cross_minus)]
  transfers between devices with their start and end apart: 13 -> 13, of which waited for: 8 -> 9; matrix products, arithmetic and copies ran while one was open for 1% -> 1% of each run, Pallas kernels for 0% -> 0%
where the time goes in v3:
time: 193 us; the launch traced here: 192 us
  waiting for transfers between devices  61.8 us (32%)
  blocking collectives  60 us (31%)
  starting transfers between devices  49.1 us (25%)
  Pallas kernels  9.3 us (5%)
  local copies, waits for them, and re-layouts  4.12 us (2%)
  between operations  4.04 us (2%)
  other arithmetic  2.61 us (1%)
    all_to_all x2, blocking collectives, spread(): lax.all_to_all(jnp.broadcast_to(value[None], (n,) + value.shape), axes, 0...  41.6 us
    all_to_all x1, blocking collectives, step(): over_x = lax.all_to_all(hidden_terms, 'x', 0, 0, tiled=True)  18.4 us
    all_to_all x2, waiting for transfers between devices, spread(): lax.all_to_all(jnp.broadcast_to(value[None], (n,) + value.shape), axes, 0...  16.3 us
    all_to_all x1, waiting for transfers between devices, step(): over_z = lax.all_to_all(over_x, 'z', 0, 0, tiled=True)  15.6 us
    all_to_all x2, starting transfers between devices, spread(): lax.all_to_all(jnp.broadcast_to(value[None], (n,) + value.shape), axes, 0...  15.3 us
    ppermute x1, waiting for transfers between devices, step(): far_pair = lax.ppermute(next_pair, 'y', minus)  10.2 us
    ppermute x1, waiting for transfers between devices, step(): prev_own = lax.ppermute(own, 'y', plus)  6.91 us
    all_to_all x1, waiting for transfers between devices, step(): terms = lax.all_to_all(terms, ('y', 'c'), 0, 0, tiled=True)  6.27 us
  transfers between devices with their start and end apart: 13, of which 9 were waited for; matrix products, arithmetic and copies ran while one was open for 1% of the time, Pallas kernels for 0%

profile of v3, /device:TPU:64, one launch (start us, length us, event | category | flops | bytes accessed | tf_op | source)
XLA Modules:
  0.0 191.7 jit_solution(4840755321794555365)
XLA Ops:
  0.6 0.8 broadcast_in_dim.38
  1.4 32.6 %all_to_all.35 = bf16[16,64,128]{2,1,0:T(8,128)(2,1)S(1)} all-to-all(bf16[16,64,128]{2,1,0:T(8,128)(2,1)S(1)} %broadcast_in_dim.38), channel_id=1, replica_groups=mesh['x'=4,'z'=16,'y'=4,'c'=2] {'z'}, dimensions={0} | all-to-all | bytes 524288 | tf_op jit(solution)/shard_map/all_to_all | solution.py:31
  34.0 1.1 broadcast_in_dim.40
  35.1 4.4 %all-to-all-start.1 = ((bf16[4,1024,128]{2,1,0:T(8,128)(2,1)}), bf16[4,1024,128]{2,1,0:T(8,128)(2,1)S(1)}, u32[]{:S(2)}, u32[]{:S(2)}) async-start(bf16[4,1024,128]{2,1,0:T(8,128)(2,1)} %broadcast_in_dim.40), calls=%async_computation.1 | async-start | bytes 2097152 | tf_op jit(solution)/shard_map/all_to_all | solution.py:31
  39.6 0.9 constant_dynamic-slice_fusion
  40.5 1.9 collective-permute-start.5
  42.4 3.6 %collective-permute-start.4 = (bf16[512,512]{1,0:T(8,128)(2,1)}, bf16[512,512]{1,0:T(8,128)(2,1)S(1)}, u32[]{:S(2)}, u32[]{:S(2)}) collective-permute-start(bf16[512,512]{1,0:T(8,128)(2,1)} %get-tuple-element.13), channel_id=1, source_target_pairs={{0,3},{1,2},{2,5},{3,4},{4,7},{5,6},{6,1},{7,0},{8,11},{9,10},{10,... | collective-permute-start | bytes 1572872 | tf_op jit(solution)/shard_map/ppermute | solution.py:229
  46.0 3.5 %collective-permute-start.2 = (bf16[512,512]{1,0:T(8,128)(2,1)S(1)}, bf16[512,512]{1,0:T(8,128)(2,1)S(1)}, u32[]{:S(2)}, u32[]{:S(2)}) collective-permute-start(bf16[512,512]{1,0:T(8,128)(2,1)S(1)} %get-tuple-element.14.refs_0_), channel_id=1, source_target_pairs={{0,2},{2,4},{4,6},{6,0},{1,3},{3,5},{5,7},{7,1},{8,10},{10,12},{12... | collective-permute-start | bytes 1572872 | tf_op jit(solution)/shard_map/ppermute | solution.py:227
  49.5 1.9 all-to-all-done.1
  51.4 1.9 collective-permute-start
  53.3 2.4 %collective-permute-start.1 = (bf16[512,512]{1,0:T(8,128)(2,1)}, bf16[512,512]{1,0:T(8,128)(2,1)}, u32[]{:S(2)}, u32[]{:S(2)}) collective-permute-start(bf16[512,512]{1,0:T(8,128)(2,1)} %get-tuple-element.13), channel_id=1, source_target_pairs={{0,1},{1,0},{2,3},{3,2},{4,5},{5,4},{6,7},{7,6},{8,9},{9,8},{10,11... | collective-permute-start | bytes 1572872 | tf_op jit(solution)/shard_map/ppermute | solution.py:232
  55.8 0.9 collective-permute-done.5.refs_5_
  56.6 4.0 %collective-permute-start.3 = (bf16[512,512]{1,0:T(8,128)(2,1)S(1)}, bf16[512,512]{1,0:T(8,128)(2,1)}, u32[]{:S(2)}, u32[]{:S(2)}) collective-permute-start(bf16[512,512]{1,0:T(8,128)(2,1)S(1)} %get-tuple-element.14.refs_0_), channel_id=1, source_target_pairs={{0,6},{2,0},{4,2},{6,4},{1,7},{3,1},{5,3},{7,5},{8,14},{10,8},{12,... | collective-permute-start | bytes 1572872 | tf_op jit(solution)/shard_map/ppermute | solution.py:228
  60.7 0.0 collective-permute-done.4.refs_4_
  60.7 4.1 %collective-permute-start.7 = (bf16[512,512]{1,0:T(8,128)(2,1)S(1)}, bf16[512,512]{1,0:T(8,128)(2,1)}, u32[]{:S(2)}, u32[]{:S(2)}) collective-permute-start(bf16[512,512]{1,0:T(8,128)(2,1)S(1)} %collective-permute-done.5.refs_5_), channel_id=1, source_target_pairs={{0,6},{2,0},{4,2},{6,4},{1,7},{3,1},{5,3},{7,5},{8,14},{10,8},{12,... | collective-permute-start | bytes 1572872 | tf_op jit(solution)/shard_map/ppermute | solution.py:231
  64.8 6.9 %collective-permute-done.2.refs_2_ = bf16[512,512]{1,0:T(8,128)(2,1)S(1)} collective-permute-done((bf16[512,512]{1,0:T(8,128)(2,1)S(1)}, bf16[512,512]{1,0:T(8,128)(2,1)S(1)}, u32[]{:S(2)}, u32[]{:S(2)}) %collective-permute-start.2) | collective-permute-done | bytes 524320 | tf_op jit(solution)/shard_map/ppermute | solution.py:227
  71.7 1.9 collective-permute-start.6
  73.6 0.1 pad_add_fusion.place
  73.7 0.0 collective-permute-done.1.refs_1_
  73.7 10.2 %collective-permute-done.7.refs_7_ = bf16[512,512]{1,0:T(8,128)(2,1)} collective-permute-done((bf16[512,512]{1,0:T(8,128)(2,1)S(1)}, bf16[512,512]{1,0:T(8,128)(2,1)}, u32[]{:S(2)}, u32[]{:S(2)}) %collective-permute-start.7) | collective-permute-done | bytes 524320 | tf_op jit(solution)/shard_map/ppermute | solution.py:231
  84.0 3.0 %collective-permute-done.6.refs_6_ = bf16[512,512]{1,0:T(8,128)(2,1)} collective-permute-done((bf16[512,512]{1,0:T(8,128)(2,1)S(1)}, bf16[512,512]{1,0:T(8,128)(2,1)}, u32[]{:S(2)}, u32[]{:S(2)}) %collective-permute-start.6) | collective-permute-done | bytes 524320 | tf_op jit(solution)/shard_map/ppermute | solution.py:230
  86.9 0.0 collective-permute-done.theirs
  86.9 4.2 %forward.1 = (bf16[16,512]{1,0:T(8,128)(2,1)S(1)}, f32[256,512]{1,0:T(8,128)S(1)}) custom-call(s32[10]{0:T(128)S(1)} %pad_add_fusion.place, bf16[4096,128]{1,0:T(8,128)(2,1)S(1)} %bitcast.17, bf16[4096,128]{1,0:T(8,128)(2,1)} %collective-permute-done.theirs, bf16[512,512]{1,0:T(8,128)(2,1)S(1)} %get-tuple-element.14.refs_0_, ...), custom_call_target="tpu_custom_call" | custom-call | flops 1073741824 | bytes 6815744 | tf_op jit(solution)/shard_map/forward/pallas_call | solution.py:79
  91.1 0.0 copy-start.5
  91.1 0.0 copy-start.6
  91.2 0.0 copy-start.7
  91.2 0.0 copy-start.1
  91.2 9.0 %all_to_all.36 = bf16[8,16,512]{2,1,0:T(8,128)(2,1)S(1)} all-to-all(bf16[8,16,512]{2,1,0:T(8,128)(2,1)S(1)} %broadcast_in_dim.41), channel_id=1, replica_groups=mesh['x'=4,'z'=16,'y'=4,'c'=2] {'y','c'}, dimensions={0} | all-to-all | bytes 262144 | tf_op jit(solution)/shard_map/all_to_all | solution.py:31
  100.2 0.3 fusion.1
  100.5 0.4 fusion
  101.0 0.7 broadcast_in_dim.43
  101.6 10.9 %all-to-all-start.3 = ((f32[64,4,128]{2,1,0:T(4,128)}), f32[64,4,128]{2,1,0:T(4,128)S(1)}, u32[]{:S(2)}, u32[]{:S(2)}) async-start(f32[64,4,128]{2,1,0:T(4,128)} %broadcast_in_dim.43), calls=%async_computation.3 | async-start | bytes 262144 | tf_op jit(solution)/shard_map/all_to_all | solution.py:31
  113.2 14.4 %all-to-all-done.3.partials = f32[64,4,128]{2,1,0:T(4,128)S(1)} async-done(((f32[64,4,128]{2,1,0:T(4,128)}), f32[64,4,128]{2,1,0:T(4,128)S(1)}, u32[]{:S(2)}, u32[]{:S(2)}) %all-to-all-start.3) | async-done | bytes 131104 | tf_op jit(solution)/shard_map/all_to_all | solution.py:31
  127.7 1.6 query_terms.1
  129.3 3.4 %all-to-all-start.4 = ((bf16[8,16,640]{2,1,0:T(8,128)(2,1)}), bf16[8,16,640]{2,1,0:T(8,128)(2,1)S(1)}, u32[]{:S(2)}, u32[]{:S(2)}) async-start(bf16[8,16,640]{2,1,0:T(8,128)(2,1)} %query_terms.1), calls=%async_computation.4 | async-start | bytes 327680 | tf_op jit(solution)/shard_map/all_to_all | solution.py:282
  132.7 0.1 divide_select_fusion.slope
  132.8 6.3 %all-to-all-done.4.terms = bf16[8,16,640]{2,1,0:T(8,128)(2,1)S(1)} async-done(((bf16[8,16,640]{2,1,0:T(8,128)(2,1)}), bf16[8,16,640]{2,1,0:T(8,128)(2,1)S(1)}, u32[]{:S(2)}, u32[]{:S(2)}) %all-to-all-start.4) | async-done | bytes 163872 | tf_op jit(solution)/shard_map/all_to_all | solution.py:282
  139.1 3.5 %backward.1 = (bf16[4096,128]{1,0:T(8,128)(2,1)S(1)}, bf16[4096,128]{1,0:T(8,128)(2,1)S(1)}, f32[1,128]{1,0:T(1,128)S(1)}) custom-call(s32[10]{0:T(128)S(1)} %pad_add_fusion.place, bf16[8,16,640]{2,1,0:T(8,128)(2,1)S(1)} %all-to-all-done.4.terms, f32[256,512]{1,0:T(8,128)S(1)} %divide_select_fusion.slope, bf16[512,512]{1,0:T(8,128)(2,1)S(1)} %get-tuple-element.14.refs_0_, ...), custom_call_target="tpu_custom_call" | custom-call | flops 1073741824 | bytes 6815744 | tf_op jit(solution)/shard_map/backward/pallas_call | solution.py:188
  142.6 1.9 %collective-permute-start.8 = (bf16[4096,128]{1,0:T(8,128)(2,1)S(1)}, bf16[4096,128]{1,0:T(8,128)(2,1)S(1)}, u32[]{:S(2)}, u32[]{:S(2)}) collective-permute-start(bf16[4096,128]{1,0:T(8,128)(2,1)S(1)} %get-tuple-element.11), channel_id=1, source_target_pairs={{0,1},{1,0},{2,3},{3,2},{4,5},{5,4},{6,7},{7,6},{8,9},{9,8},{10,11... | collective-permute-start | bytes 3145736 | tf_op jit(solution)/shard_map/ppermute | solution.py:286
  144.5 2.6 %collective-permute-done.8 = bf16[4096,128]{1,0:T(8,128)(2,1)S(1)} collective-permute-done((bf16[4096,128]{1,0:T(8,128)(2,1)S(1)}, bf16[4096,128]{1,0:T(8,128)(2,1)S(1)}, u32[]{:S(2)}, u32[]{:S(2)}) %collective-permute-start.8) | collective-permute-done | bytes 1048608 | tf_op jit(solution)/shard_map/ppermute | solution.py:286
  147.2 0.3 add_convert_fusion
  147.4 18.4 %all_to_all.37 = bf16[4,1024,128]{2,1,0:T(8,128)(2,1)S(1)} all-to-all(bf16[4,1024,128]{2,1,0:T(8,128)(2,1)S(1)} %bitcast.18), channel_id=1, replica_groups=mesh['x'=4,'z'=16,'y'=4,'c'=2] {'x'}, dimensions={0} | all-to-all | bytes 2097152 | tf_op jit(solution)/shard_map/all_to_all | solution.py:289
  165.8 0.9 reduce_sum.34
  166.7 5.1 %all-to-all-start.6 = ((bf16[16,64,128]{2,1,0:T(8,128)(2,1)}), bf16[16,64,128]{2,1,0:T(8,128)(2,1)S(1)}, u32[]{:S(2)}, u32[]{:S(2)}) async-start(bf16[16,64,128]{2,1,0:T(8,128)(2,1)} %bitcast.10), calls=%async_computation.6 | async-start | bytes 524288 | tf_op jit(solution)/shard_map/all_to_all | solution.py:291
  171.8 0.6 fusion.3
  172.4 0.6 fusion.11
  174.3 15.6 %all-to-all-done.6 = bf16[16,64,128]{2,1,0:T(8,128)(2,1)S(1)} async-done(((bf16[16,64,128]{2,1,0:T(8,128)(2,1)}), bf16[16,64,128]{2,1,0:T(8,128)(2,1)S(1)}, u32[]{:S(2)}, u32[]{:S(2)}) %all-to-all-start.6) | async-done | bytes 262176 | tf_op jit(solution)/shard_map/all_to_all | solution.py:291
  189.9 0.6 reduce_sum.35
  (24 shorter events, 0.1 us)
Async XLA Ops:
  35.1 4.4 %copy-start.4 = (bf16[512,1024]{1,0:T(8,128)(2,1)S(1)}, bf16[512,1024]{1,0:T(8,128)(2,1)}, u32[]{:S(2)}) copy-start(bf16[512,1024]{1,0:T(8,128)(2,1)} %param.10) | copy-start | bytes 3145732
  35.1 16.3 %all-to-all-start.1 = ((bf16[4,1024,128]{2,1,0:T(8,128)(2,1)}), bf16[4,1024,128]{2,1,0:T(8,128)(2,1)S(1)}, u32[]{:S(2)}, u32[]{:S(2)}) async-start(bf16[4,1024,128]{2,1,0:T(8,128)(2,1)} %broadcast_in_dim.40), calls=%async_computation.1 | async-start | bytes 2097152 | tf_op jit(solution)/shard_map/all_to_all | solution.py:31
  39.6 34.0 %copy-start.8 = (s32[8]{0:T(128)S(1)}, s32[8]{0:T(128)}, u32[]{:S(2)}) copy-start(s32[8]{0:T(128)} %constant.65.clone) | copy-start | bytes 100
  39.6 34.0 %copy-start.9 = (s32[8]{0:T(128)S(1)}, s32[8]{0:T(128)}, u32[]{:S(2)}) copy-start(s32[8]{0:T(128)} %constant.64.clone) | copy-start | bytes 100
  40.5 16.2 %collective-permute-start.5 = (bf16[512,512]{1,0:T(8,128)(2,1)}, bf16[512,512]{1,0:T(8,128)(2,1)S(1)}, u32[]{:S(2)}, u32[]{:S(2)}) collective-permute-start(bf16[512,512]{1,0:T(8,128)(2,1)} %get-tuple-element.13), channel_id=1, source_target_pairs={{0,7},{1,6},{2,1},{3,0},{4,3},{5,2},{6,5},{7,4},{8,15},{9,14},{10,... | collective-permute-start | bytes 1572872 | tf_op jit(solution)/shard_map/ppermute | solution.py:226
  42.4 18.3 %collective-permute-start.4 = (bf16[512,512]{1,0:T(8,128)(2,1)}, bf16[512,512]{1,0:T(8,128)(2,1)S(1)}, u32[]{:S(2)}, u32[]{:S(2)}) collective-permute-start(bf16[512,512]{1,0:T(8,128)(2,1)} %get-tuple-element.13), channel_id=1, source_target_pairs={{0,3},{1,2},{2,5},{3,4},{4,7},{5,6},{6,1},{7,0},{8,11},{9,10},{10,... | collective-permute-start | bytes 1572872 | tf_op jit(solution)/shard_map/ppermute | solution.py:229
  46.0 25.6 %collective-permute-start.2 = (bf16[512,512]{1,0:T(8,128)(2,1)S(1)}, bf16[512,512]{1,0:T(8,128)(2,1)S(1)}, u32[]{:S(2)}, u32[]{:S(2)}) collective-permute-start(bf16[512,512]{1,0:T(8,128)(2,1)S(1)} %get-tuple-element.14.refs_0_), channel_id=1, source_target_pairs={{0,2},{2,4},{4,6},{6,0},{1,3},{3,5},{5,7},{7,1},{8,10},{10,12},{12... | collective-permute-start | bytes 1572872 | tf_op jit(solution)/shard_map/ppermute | solution.py:227
  51.4 35.5 %collective-permute-start = (bf16[4096,128]{1,0:T(8,128)(2,1)S(1)}, bf16[4096,128]{1,0:T(8,128)(2,1)}, u32[]{:S(2)}, u32[]{:S(2)}) collective-permute-start(bf16[4096,128]{1,0:T(8,128)(2,1)S(1)} %bitcast.16), channel_id=1, source_target_pairs={{0,1},{1,0},{2,3},{3,2},{4,5},{5,4},{6,7},{7,6},{8,9},{9,8},{10,11... | collective-permute-start | bytes 3145736 | tf_op jit(solution)/shard_map/ppermute | solution.py:236
  53.3 20.4 %collective-permute-start.1 = (bf16[512,512]{1,0:T(8,128)(2,1)}, bf16[512,512]{1,0:T(8,128)(2,1)}, u32[]{:S(2)}, u32[]{:S(2)}) collective-permute-start(bf16[512,512]{1,0:T(8,128)(2,1)} %get-tuple-element.13), channel_id=1, source_target_pairs={{0,1},{1,0},{2,3},{3,2},{4,5},{5,4},{6,7},{7,6},{8,9},{9,8},{10,11... | collective-permute-start | bytes 1572872 | tf_op jit(solution)/shard_map/ppermute | solution.py:232
  56.6 17.1 %collective-permute-start.3 = (bf16[512,512]{1,0:T(8,128)(2,1)S(1)}, bf16[512,512]{1,0:T(8,128)(2,1)}, u32[]{:S(2)}, u32[]{:S(2)}) collective-permute-start(bf16[512,512]{1,0:T(8,128)(2,1)S(1)} %get-tuple-element.14.refs_0_), channel_id=1, source_target_pairs={{0,6},{2,0},{4,2},{6,4},{1,7},{3,1},{5,3},{7,5},{8,14},{10,8},{12,... | collective-permute-start | bytes 1572872 | tf_op jit(solution)/shard_map/ppermute | solution.py:228
  60.7 23.2 %collective-permute-start.7 = (bf16[512,512]{1,0:T(8,128)(2,1)S(1)}, bf16[512,512]{1,0:T(8,128)(2,1)}, u32[]{:S(2)}, u32[]{:S(2)}) collective-permute-start(bf16[512,512]{1,0:T(8,128)(2,1)S(1)} %collective-permute-done.5.refs_5_), channel_id=1, source_target_pairs={{0,6},{2,0},{4,2},{6,4},{1,7},{3,1},{5,3},{7,5},{8,14},{10,8},{12,... | collective-permute-start | bytes 1572872 | tf_op jit(solution)/shard_map/ppermute | solution.py:231
  71.7 15.2 %collective-permute-start.6 = (bf16[512,512]{1,0:T(8,128)(2,1)S(1)}, bf16[512,512]{1,0:T(8,128)(2,1)}, u32[]{:S(2)}, u32[]{:S(2)}) collective-permute-start(bf16[512,512]{1,0:T(8,128)(2,1)S(1)} %collective-permute-done.2.refs_2_), channel_id=1, source_target_pairs={{0,2},{2,4},{4,6},{6,0},{1,3},{3,5},{5,7},{7,1},{8,10},{10,12},{12... | collective-permute-start | bytes 1572872 | tf_op jit(solution)/shard_map/ppermute | solution.py:230
  73.7 26.5 %copy-start = (bf16[256,1024]{1,0:T(8,128)(2,1)S(1)}, bf16[256,1024]{1,0:T(8,128)(2,1)}, u32[]{:S(2)}) copy-start(bf16[256,1024]{1,0:T(8,128)(2,1)} %stored.1) | copy-start | bytes 1572868
  91.1 9.4 %copy-start.2 = (f32[256,512]{1,0:T(8,128)}, f32[256,512]{1,0:T(8,128)S(1)}, u32[]{:S(2)}) copy-start(f32[256,512]{1,0:T(8,128)S(1)} %get-tuple-element.9) | copy-start | bytes 1572868
  91.1 9.4 %copy-start.5 = (s32[384]{0:T(512)S(1)}, s32[384]{0:T(512)}, u32[]{:S(2)}) copy-start(s32[384]{0:T(512)} %param.12) | copy-start | bytes 4612
  91.1 9.4 %copy-start.6 = (s32[384]{0:T(512)S(1)}, s32[384]{0:T(512)}, u32[]{:S(2)}) copy-start(s32[384]{0:T(512)} %param.13) | copy-start | bytes 4612
  91.2 22.1 %copy-start.7 = (f32[384]{0:T(512)S(1)}, f32[384]{0:T(512)}, u32[]{:S(2)}) copy-start(f32[384]{0:T(512)} %param.15) | copy-start | bytes 4612
  91.2 36.5 %copy-start.1 = (bf16[256,1024]{1,0:T(8,128)(2,1)S(1)}, bf16[256,1024]{1,0:T(8,128)(2,1)}, u32[]{:S(2)}) copy-start(bf16[256,1024]{1,0:T(8,128)(2,1)} %stored.1) | copy-start | bytes 1572868
  100.9 31.8 %copy-start.3 = (f32[256,512]{1,0:T(8,128)S(1)}, f32[256,512]{1,0:T(8,128)}, u32[]{:S(2)}) copy-start(f32[256,512]{1,0:T(8,128)} %copy-done.2) | copy-start | bytes 1572868
  101.6 26.0 %all-to-all-start.3 = ((f32[64,4,128]{2,1,0:T(4,128)}), f32[64,4,128]{2,1,0:T(4,128)S(1)}, u32[]{:S(2)}, u32[]{:S(2)}) async-start(f32[64,4,128]{2,1,0:T(4,128)} %broadcast_in_dim.43), calls=%async_computation.3 | async-start | bytes 262144 | tf_op jit(solution)/shard_map/all_to_all | solution.py:31
  129.3 9.8 %all-to-all-start.4 = ((bf16[8,16,640]{2,1,0:T(8,128)(2,1)}), bf16[8,16,640]{2,1,0:T(8,128)(2,1)S(1)}, u32[]{:S(2)}, u32[]{:S(2)}) async-start(bf16[8,16,640]{2,1,0:T(8,128)(2,1)} %query_terms.1), calls=%async_computation.4 | async-start | bytes 327680 | tf_op jit(solution)/shard_map/all_to_all | solution.py:282
  142.6 4.6 %collective-permute-start.8 = (bf16[4096,128]{1,0:T(8,128)(2,1)S(1)}, bf16[4096,128]{1,0:T(8,128)(2,1)S(1)}, u32[]{:S(2)}, u32[]{:S(2)}) collective-permute-start(bf16[4096,128]{1,0:T(8,128)(2,1)S(1)} %get-tuple-element.11), channel_id=1, source_target_pairs={{0,1},{1,0},{2,3},{3,2},{4,5},{5,4},{6,7},{7,6},{8,9},{9,8},{10,11... | collective-permute-start | bytes 3145736 | tf_op jit(solution)/shard_map/ppermute | solution.py:286
  166.7 23.2 %all-to-all-start.6 = ((bf16[16,64,128]{2,1,0:T(8,128)(2,1)}), bf16[16,64,128]{2,1,0:T(8,128)(2,1)S(1)}, u32[]{:S(2)}, u32[]{:S(2)}) async-start(bf16[16,64,128]{2,1,0:T(8,128)(2,1)} %bitcast.10), calls=%async_computation.6 | async-start | bytes 524288 | tf_op jit(solution)/shard_map/all_to_all | solution.py:291

commit v4 on v3

--- a/solution.py
+++ b/solution.py
@@ -44,24 +44,27 @@
     blocks, (pooled, logits, feats, held, total, sems) = refs[:nb], refs[nb:]
     rows = held.shape[1]
     tok = mine.shape[1]
-    copies = [
-        pltpu.make_async_copy(mine, feats.at[:, pl.ds(0, tok)], sems.at[nb]),
-        pltpu.make_async_copy(theirs, feats.at[:, pl.ds(tok, tok)], sems.at[nb + 1]),
-    ]
-    copies += [pltpu.make_async_copy(blocks[k], held.at[k], sems.at[k]) for k in range(nb)]
+    copies = []
+    for k in range(nb):
+        start = pl.multiple_of(place[k], rows)
+        near = feats.at[k, :, pl.ds(0, tok)]
+        far = feats.at[k, :, pl.ds(tok, tok)]
+        copies += [
+            pltpu.make_async_copy(blocks[k], held.at[k], sems.at[k]),
+            pltpu.make_async_copy(mine.at[pl.ds(start, rows)], near, sems.at[nb + k]),
+            pltpu.make_async_copy(theirs.at[pl.ds(start, rows)], far, sems.at[2 * nb + k]),
+        ]
     for copy in copies:
         copy.start()
-    copies[0].wait()
-    copies[1].wait()
     for k in range(nb):
-        copies[2 + k].wait()
-        start = pl.multiple_of(place[k], rows)
-        term = dot(feats[pl.ds(start, rows), :], held[k], 0, 0)
+        for copy in copies[3 * k : 3 * k + 3]:
+            copy.wait()
+        term = dot(feats[k], held[k], 0, 0)
         if k:
             total[...] += term
         else:
             total[...] = term
-    keep = pltpu.make_async_copy(total, logits, sems.at[nb + 2])
+    keep = pltpu.make_async_copy(total, logits, sems.at[3 * nb])
     keep.start()
     sums = jnp.log1p(jnp.maximum(total[...], 0.0)).reshape(-1, QLEN, total.shape[1]).sum(1)
     half = sums.shape[0] // 2
@@ -86,10 +89,10 @@
         in_specs=[SMEM] + [ANY] * (2 + nb),
         out_specs=(WHOLE, ANY),
         scratch_shapes=[
-            pltpu.VMEM((depth, 2 * tok), BF16),
+            pltpu.VMEM((nb, rows, 2 * tok), BF16),
             pltpu.VMEM((nb, rows, cols), BF16),
             pltpu.VMEM((2 * tok, cols), F32),
-            pltpu.SemaphoreType.DMA((nb + 3,)),
+            pltpu.SemaphoreType.DMA((3 * nb + 1,)),
         ],
         cost_estimate=pl.CostEstimate(
             flops=4 * tok * depth * cols,
@@ -110,7 +113,7 @@
     cores = passages.shape[1] // half
     slots = pair_query.shape[1]
     inv_root = 1.0 / math.sqrt(VOCAB)
-    total = partials[...].sum(0)
+    total = partials[...].astype(F32).sum(0)
     lines = slots // LANES
     scores = jnp.concatenate([total[i : i + 1] for i in range(lines)], axis=1) * inv_root
     is_live = lax.broadcasted_iota(jnp.int32, (1, slots), 1) < pair_count[0]
@@ -265,7 +268,7 @@
     passage_hot = (pair_passage == jnp.arange(n_passage, dtype=jnp.int32)[:, None]).astype(F32)
     spread_table = jnp.dot(table, query_hot, precision=lax.Precision.HIGHEST)
     partial_value = (spread_table * passage_hot).sum(0)
-    packed = jnp.pad(partial_value, (0, -slots % 512)).reshape(-1, LANES)
+    packed = jnp.pad(partial_value, (0, -slots % 512)).reshape(-1, LANES).astype(BF16)
     partials = spread(packed, ("x", "z"), nx * nz)
     positive = jnp.maximum(logits, 0.0)
     slope = jnp.where(logits > 0, 1.0 / (1.0 + positive), 0.0)

time: 193 us -> 191 us (0.990)
  the two profiles are of different devices: /device:TPU:64 before, /device:TPU:32 now
where the time goes in v4:
time: 191 us; the launch traced here: 190 us
  waiting for transfers between devices  61.8 us (32%)
  blocking collectives  60.1 us (31%)
  starting transfers between devices  47.5 us (25%)
  Pallas kernels  8.98 us (5%)
  local copies, waits for them, and re-layouts  4.08 us (2%)
  between operations  4.04 us (2%)
  other arithmetic  2.61 us (1%)
    all_to_all x2, blocking collectives, spread(): lax.all_to_all(jnp.broadcast_to(value[None], (n,) + value.shape), axes, 0...  42 us
    all_to_all x1, blocking collectives, step(): over_x = lax.all_to_all(hidden_terms, 'x', 0, 0, tiled=True)  18.1 us
    all_to_all x2, waiting for transfers between devices, spread(): lax.all_to_all(jnp.broadcast_to(value[None], (n,) + value.shape), axes, 0...  17.4 us
    all_to_all x1, waiting for transfers between devices, step(): over_z = lax.all_to_all(over_x, 'z', 0, 0, tiled=True)  15.6 us
    all_to_all x2, starting transfers between devices, spread(): lax.all_to_all(jnp.broadcast_to(value[None], (n,) + value.shape), axes, 0...  14.6 us
    ppermute x1, waiting for transfers between devices, step(): far_pair = lax.ppermute(next_pair, 'y', minus)  10.3 us
    ppermute x1, waiting for transfers between devices, step(): prev_own = lax.ppermute(own, 'y', plus)  6.71 us
    all_to_all x1, waiting for transfers between devices, step(): terms = lax.all_to_all(terms, ('y', 'c'), 0, 0, tiled=True)  6.27 us
  transfers between devices with their start and end apart: 13, of which 9 were waited for; matrix products, arithmetic and copies ran while one was open for 1% of the time, Pallas kernels for 0%

profile of v4, /device:TPU:32, one launch (start us, length us, event | category | flops | bytes accessed | tf_op | source)
XLA Modules:
  0.0 189.8 jit_solution(9509865690069057626)
XLA Ops:
  0.6 0.8 broadcast_in_dim.17
  1.4 32.9 %all_to_all.35 = bf16[16,64,128]{2,1,0:T(8,128)(2,1)S(1)} all-to-all(bf16[16,64,128]{2,1,0:T(8,128)(2,1)S(1)} %broadcast_in_dim.17), channel_id=1, replica_groups=mesh['x'=4,'z'=16,'y'=4,'c'=2] {'z'}, dimensions={0} | all-to-all | bytes 524288 | tf_op jit(solution)/shard_map/all_to_all | solution.py:31
  34.3 1.1 broadcast_in_dim.19
  35.5 4.4 %all-to-all-start.1 = ((bf16[4,1024,128]{2,1,0:T(8,128)(2,1)}), bf16[4,1024,128]{2,1,0:T(8,128)(2,1)S(1)}, u32[]{:S(2)}, u32[]{:S(2)}) async-start(bf16[4,1024,128]{2,1,0:T(8,128)(2,1)} %broadcast_in_dim.19), calls=%async_computation.1 | async-start | bytes 2097152 | tf_op jit(solution)/shard_map/all_to_all | solution.py:31
  39.9 0.9 constant_dynamic-slice_fusion
  40.8 3.3 %collective-permute-start.5 = (bf16[512,512]{1,0:T(8,128)(2,1)}, bf16[512,512]{1,0:T(8,128)(2,1)S(1)}, u32[]{:S(2)}, u32[]{:S(2)}) collective-permute-start(bf16[512,512]{1,0:T(8,128)(2,1)} %get-tuple-element.13), channel_id=1, source_target_pairs={{0,7},{1,6},{2,1},{3,0},{4,3},{5,2},{6,5},{7,4},{8,15},{9,14},{10,... | collective-permute-start | bytes 1572872 | tf_op jit(solution)/shard_map/ppermute | solution.py:229
  44.1 2.3 %collective-permute-start.4 = (bf16[512,512]{1,0:T(8,128)(2,1)}, bf16[512,512]{1,0:T(8,128)(2,1)S(1)}, u32[]{:S(2)}, u32[]{:S(2)}) collective-permute-start(bf16[512,512]{1,0:T(8,128)(2,1)} %get-tuple-element.13), channel_id=1, source_target_pairs={{0,3},{1,2},{2,5},{3,4},{4,7},{5,6},{6,1},{7,0},{8,11},{9,10},{10,... | collective-permute-start | bytes 1572872 | tf_op jit(solution)/shard_map/ppermute | solution.py:232
  46.3 3.5 %collective-permute-start.2 = (bf16[512,512]{1,0:T(8,128)(2,1)S(1)}, bf16[512,512]{1,0:T(8,128)(2,1)S(1)}, u32[]{:S(2)}, u32[]{:S(2)}) collective-permute-start(bf16[512,512]{1,0:T(8,128)(2,1)S(1)} %get-tuple-element.14.refs_0_), channel_id=1, source_target_pairs={{0,2},{2,4},{4,6},{6,0},{1,3},{3,5},{5,7},{7,1},{8,10},{10,12},{12... | collective-permute-start | bytes 1572872 | tf_op jit(solution)/shard_map/ppermute | solution.py:230
  49.8 4.3 %all-to-all-done.1 = bf16[4,1024,128]{2,1,0:T(8,128)(2,1)S(1)} async-done(((bf16[4,1024,128]{2,1,0:T(8,128)(2,1)}), bf16[4,1024,128]{2,1,0:T(8,128)(2,1)S(1)}, u32[]{:S(2)}, u32[]{:S(2)}) %all-to-all-start.1) | async-done | bytes 1048608 | tf_op jit(solution)/shard_map/all_to_all | solution.py:31
  54.2 1.9 %collective-permute-start = (bf16[4096,128]{1,0:T(8,128)(2,1)S(1)}, bf16[4096,128]{1,0:T(8,128)(2,1)}, u32[]{:S(2)}, u32[]{:S(2)}) collective-permute-start(bf16[4096,128]{1,0:T(8,128)(2,1)S(1)} %bitcast.16), channel_id=1, source_target_pairs={{0,1},{1,0},{2,3},{3,2},{4,5},{5,4},{6,7},{7,6},{8,9},{9,8},{10,11... | collective-permute-start | bytes 3145736 | tf_op jit(solution)/shard_map/ppermute | solution.py:239
  56.1 2.4 %collective-permute-start.1 = (bf16[512,512]{1,0:T(8,128)(2,1)}, bf16[512,512]{1,0:T(8,128)(2,1)}, u32[]{:S(2)}, u32[]{:S(2)}) collective-permute-start(bf16[512,512]{1,0:T(8,128)(2,1)} %get-tuple-element.13), channel_id=1, source_target_pairs={{0,1},{1,0},{2,3},{3,2},{4,5},{5,4},{6,7},{7,6},{8,9},{9,8},{10,11... | collective-permute-start | bytes 1572872 | tf_op jit(solution)/shard_map/ppermute | solution.py:235
  58.5 0.0 collective-permute-done.5.refs_5_
  58.5 4.9 %collective-permute-start.3 = (bf16[512,512]{1,0:T(8,128)(2,1)S(1)}, bf16[512,512]{1,0:T(8,128)(2,1)}, u32[]{:S(2)}, u32[]{:S(2)}) collective-permute-start(bf16[512,512]{1,0:T(8,128)(2,1)S(1)} %get-tuple-element.14.refs_0_), channel_id=1, source_target_pairs={{0,6},{2,0},{4,2},{6,4},{1,7},{3,1},{5,3},{7,5},{8,14},{10,8},{12,... | collective-permute-start | bytes 1572872 | tf_op jit(solution)/shard_map/ppermute | solution.py:231
  63.5 2.7 %collective-permute-start.7 = (bf16[512,512]{1,0:T(8,128)(2,1)S(1)}, bf16[512,512]{1,0:T(8,128)(2,1)}, u32[]{:S(2)}, u32[]{:S(2)}) collective-permute-start(bf16[512,512]{1,0:T(8,128)(2,1)S(1)} %collective-permute-done.5.refs_5_), channel_id=1, source_target_pairs={{0,6},{2,0},{4,2},{6,4},{1,7},{3,1},{5,3},{7,5},{8,14},{10,8},{12,... | collective-permute-start | bytes 1572872 | tf_op jit(solution)/shard_map/ppermute | solution.py:234
  66.1 6.7 %collective-permute-done.2.refs_2_ = bf16[512,512]{1,0:T(8,128)(2,1)S(1)} collective-permute-done((bf16[512,512]{1,0:T(8,128)(2,1)S(1)}, bf16[512,512]{1,0:T(8,128)(2,1)S(1)}, u32[]{:S(2)}, u32[]{:S(2)}) %collective-permute-start.2) | collective-permute-done | bytes 524320 | tf_op jit(solution)/shard_map/ppermute | solution.py:230
  72.8 1.9 %collective-permute-start.6 = (bf16[512,512]{1,0:T(8,128)(2,1)S(1)}, bf16[512,512]{1,0:T(8,128)(2,1)}, u32[]{:S(2)}, u32[]{:S(2)}) collective-permute-start(bf16[512,512]{1,0:T(8,128)(2,1)S(1)} %collective-permute-done.2.refs_2_), channel_id=1, source_target_pairs={{0,2},{2,4},{4,6},{6,0},{1,3},{3,5},{5,7},{7,1},{8,10},{10,12},{12... | collective-permute-start | bytes 1572872 | tf_op jit(solution)/shard_map/ppermute | solution.py:233
  74.8 0.1 pad_add_fusion.place
  74.9 0.0 collective-permute-done.1.refs_1_
  74.9 0.9 collective-permute-done.3.refs_3_
  75.7 10.3 %collective-permute-done.7.refs_7_ = bf16[512,512]{1,0:T(8,128)(2,1)} collective-permute-done((bf16[512,512]{1,0:T(8,128)(2,1)S(1)}, bf16[512,512]{1,0:T(8,128)(2,1)}, u32[]{:S(2)}, u32[]{:S(2)}) %collective-permute-start.7) | collective-permute-done | bytes 524320 | tf_op jit(solution)/shard_map/ppermute | solution.py:234
  86.0 2.0 %collective-permute-done.6.refs_6_ = bf16[512,512]{1,0:T(8,128)(2,1)} collective-permute-done((bf16[512,512]{1,0:T(8,128)(2,1)S(1)}, bf16[512,512]{1,0:T(8,128)(2,1)}, u32[]{:S(2)}, u32[]{:S(2)}) %collective-permute-start.6) | collective-permute-done | bytes 524320 | tf_op jit(solution)/shard_map/ppermute | solution.py:233
  88.0 0.0 collective-permute-done.theirs
  88.0 3.9 %forward.1 = (bf16[16,512]{1,0:T(8,128)(2,1)S(1)}, f32[256,512]{1,0:T(8,128)S(1)}) custom-call(s32[10]{0:T(128)S(1)} %pad_add_fusion.place, bf16[4096,128]{1,0:T(8,128)(2,1)S(1)} %bitcast.17, bf16[4096,128]{1,0:T(8,128)(2,1)} %collective-permute-done.theirs, bf16[512,512]{1,0:T(8,128)(2,1)S(1)} %get-tuple-element.14.refs_0_, ...), custom_call_target="tpu_custom_call" | custom-call | flops 1073741824 | bytes 6815744 | tf_op jit(solution)/shard_map/forward/pallas_call | solution.py:82
  91.9 0.0 copy-start.5
  91.9 0.0 copy-start.6
  91.9 0.0 copy-start.7
  92.0 0.0 copy-start.1
  92.0 9.1 %all_to_all.36 = bf16[8,16,512]{2,1,0:T(8,128)(2,1)S(1)} all-to-all(bf16[8,16,512]{2,1,0:T(8,128)(2,1)S(1)} %broadcast_in_dim.40), channel_id=1, replica_groups=mesh['x'=4,'z'=16,'y'=4,'c'=2] {'y','c'}, dimensions={0} | all-to-all | bytes 262144 | tf_op jit(solution)/shard_map/all_to_all | solution.py:31
  101.1 0.3 fusion.1
  101.4 0.4 fusion
  101.8 0.6 broadcast_in_dim.41
  102.5 10.2 %all-to-all-start.3 = ((bf16[64,4,128]{2,1,0:T(4,128)(2,1)}), bf16[64,4,128]{2,1,0:T(4,128)(2,1)S(1)}, u32[]{:S(2)}, u32[]{:S(2)}) async-start(bf16[64,4,128]{2,1,0:T(4,128)(2,1)} %broadcast_in_dim.41), calls=%async_computation.3 | async-start | bytes 131072 | tf_op jit(solution)/shard_map/all_to_all | solution.py:31
  113.4 13.1 %all-to-all-done.3.partials = bf16[64,4,128]{2,1,0:T(4,128)(2,1)S(1)} async-done(((bf16[64,4,128]{2,1,0:T(4,128)(2,1)}), bf16[64,4,128]{2,1,0:T(4,128)(2,1)S(1)}, u32[]{:S(2)}, u32[]{:S(2)}) %all-to-all-start.3) | async-done | bytes 65568 | tf_op jit(solution)/shard_map/all_to_all | solution.py:31
  126.5 1.6 query_terms.1
  128.1 3.4 %all-to-all-start.4 = ((bf16[8,16,640]{2,1,0:T(8,128)(2,1)}), bf16[8,16,640]{2,1,0:T(8,128)(2,1)S(1)}, u32[]{:S(2)}, u32[]{:S(2)}) async-start(bf16[8,16,640]{2,1,0:T(8,128)(2,1)} %query_terms.1), calls=%async_computation.4 | async-start | bytes 327680 | tf_op jit(solution)/shard_map/all_to_all | solution.py:285
  131.5 0.1 divide_select_fusion.slope
  131.6 6.3 %all-to-all-done.4.terms = bf16[8,16,640]{2,1,0:T(8,128)(2,1)S(1)} async-done(((bf16[8,16,640]{2,1,0:T(8,128)(2,1)}), bf16[8,16,640]{2,1,0:T(8,128)(2,1)S(1)}, u32[]{:S(2)}, u32[]{:S(2)}) %all-to-all-start.4) | async-done | bytes 163872 | tf_op jit(solution)/shard_map/all_to_all | solution.py:285
  137.9 3.5 %backward.1 = (bf16[4096,128]{1,0:T(8,128)(2,1)S(1)}, bf16[4096,128]{1,0:T(8,128)(2,1)S(1)}, f32[1,128]{1,0:T(1,128)S(1)}) custom-call(s32[10]{0:T(128)S(1)} %pad_add_fusion.place, bf16[8,16,640]{2,1,0:T(8,128)(2,1)S(1)} %all-to-all-done.4.terms, f32[256,512]{1,0:T(8,128)S(1)} %divide_select_fusion.slope, bf16[512,512]{1,0:T(8,128)(2,1)S(1)} %get-tuple-element.14.refs_0_, ...), custom_call_target="tpu_custom_call" | custom-call | flops 1073741824 | bytes 6815744 | tf_op jit(solution)/shard_map/backward/pallas_call | solution.py:191
  141.4 1.9 %collective-permute-start.8 = (bf16[4096,128]{1,0:T(8,128)(2,1)S(1)}, bf16[4096,128]{1,0:T(8,128)(2,1)S(1)}, u32[]{:S(2)}, u32[]{:S(2)}) collective-permute-start(bf16[4096,128]{1,0:T(8,128)(2,1)S(1)} %get-tuple-element.11), channel_id=1, source_target_pairs={{0,1},{1,0},{2,3},{3,2},{4,5},{5,4},{6,7},{7,6},{8,9},{9,8},{10,11... | collective-permute-start | bytes 3145736 | tf_op jit(solution)/shard_map/ppermute | solution.py:289
  143.3 2.6 %collective-permute-done.8 = bf16[4096,128]{1,0:T(8,128)(2,1)S(1)} collective-permute-done((bf16[4096,128]{1,0:T(8,128)(2,1)S(1)}, bf16[4096,128]{1,0:T(8,128)(2,1)S(1)}, u32[]{:S(2)}, u32[]{:S(2)}) %collective-permute-start.8) | collective-permute-done | bytes 1048608 | tf_op jit(solution)/shard_map/ppermute | solution.py:289
  145.9 0.3 add_convert_fusion
  146.2 18.1 %all_to_all.37 = bf16[4,1024,128]{2,1,0:T(8,128)(2,1)S(1)} all-to-all(bf16[4,1024,128]{2,1,0:T(8,128)(2,1)S(1)} %bitcast.18), channel_id=1, replica_groups=mesh['x'=4,'z'=16,'y'=4,'c'=2] {'x'}, dimensions={0} | all-to-all | bytes 2097152 | tf_op jit(solution)/shard_map/all_to_all | solution.py:292
  164.3 0.9 reduce_sum.34
  165.2 4.7 %all-to-all-start.6 = ((bf16[16,64,128]{2,1,0:T(8,128)(2,1)}), bf16[16,64,128]{2,1,0:T(8,128)(2,1)S(1)}, u32[]{:S(2)}, u32[]{:S(2)}) async-start(bf16[16,64,128]{2,1,0:T(8,128)(2,1)} %bitcast.10), calls=%async_computation.6 | async-start | bytes 524288 | tf_op jit(solution)/shard_map/all_to_all | solution.py:294
  169.9 0.6 fusion.3
  170.5 0.6 fusion.11
  172.4 15.6 %all-to-all-done.6 = bf16[16,64,128]{2,1,0:T(8,128)(2,1)S(1)} async-done(((bf16[16,64,128]{2,1,0:T(8,128)(2,1)}), bf16[16,64,128]{2,1,0:T(8,128)(2,1)S(1)}, u32[]{:S(2)}, u32[]{:S(2)}) %all-to-all-start.6) | async-done | bytes 262176 | tf_op jit(solution)/shard_map/all_to_all | solution.py:294
  188.0 0.6 reduce_sum.35
  (24 shorter events, 0.1 us)
Async XLA Ops:
  35.5 4.4 %copy-start.4 = (bf16[512,1024]{1,0:T(8,128)(2,1)S(1)}, bf16[512,1024]{1,0:T(8,128)(2,1)}, u32[]{:S(2)}) copy-start(bf16[512,1024]{1,0:T(8,128)(2,1)} %param.10) | copy-start | bytes 3145732
  35.5 18.7 %all-to-all-start.1 = ((bf16[4,1024,128]{2,1,0:T(8,128)(2,1)}), bf16[4,1024,128]{2,1,0:T(8,128)(2,1)S(1)}, u32[]{:S(2)}, u32[]{:S(2)}) async-start(bf16[4,1024,128]{2,1,0:T(8,128)(2,1)} %broadcast_in_dim.19), calls=%async_computation.1 | async-start | bytes 2097152 | tf_op jit(solution)/shard_map/all_to_all | solution.py:31
  39.9 34.9 %copy-start.8 = (s32[8]{0:T(128)S(1)}, s32[8]{0:T(128)}, u32[]{:S(2)}) copy-start(s32[8]{0:T(128)} %constant.66.clone) | copy-start | bytes 100
  39.9 34.9 %copy-start.9 = (s32[8]{0:T(128)S(1)}, s32[8]{0:T(128)}, u32[]{:S(2)}) copy-start(s32[8]{0:T(128)} %constant.65.clone) | copy-start | bytes 100
  40.8 17.7 %collective-permute-start.5 = (bf16[512,512]{1,0:T(8,128)(2,1)}, bf16[512,512]{1,0:T(8,128)(2,1)S(1)}, u32[]{:S(2)}, u32[]{:S(2)}) collective-permute-start(bf16[512,512]{1,0:T(8,128)(2,1)} %get-tuple-element.13), channel_id=1, source_target_pairs={{0,7},{1,6},{2,1},{3,0},{4,3},{5,2},{6,5},{7,4},{8,15},{9,14},{10,... | collective-permute-start | bytes 1572872 | tf_op jit(solution)/shard_map/ppermute | solution.py:229
  44.1 19.4 %collective-permute-start.4 = (bf16[512,512]{1,0:T(8,128)(2,1)}, bf16[512,512]{1,0:T(8,128)(2,1)S(1)}, u32[]{:S(2)}, u32[]{:S(2)}) collective-permute-start(bf16[512,512]{1,0:T(8,128)(2,1)} %get-tuple-element.13), channel_id=1, source_target_pairs={{0,3},{1,2},{2,5},{3,4},{4,7},{5,6},{6,1},{7,0},{8,11},{9,10},{10,... | collective-permute-start | bytes 1572872 | tf_op jit(solution)/shard_map/ppermute | solution.py:232
  46.3 26.5 %collective-permute-start.2 = (bf16[512,512]{1,0:T(8,128)(2,1)S(1)}, bf16[512,512]{1,0:T(8,128)(2,1)S(1)}, u32[]{:S(2)}, u32[]{:S(2)}) collective-permute-start(bf16[512,512]{1,0:T(8,128)(2,1)S(1)} %get-tuple-element.14.refs_0_), channel_id=1, source_target_pairs={{0,2},{2,4},{4,6},{6,0},{1,3},{3,5},{5,7},{7,1},{8,10},{10,12},{12... | collective-permute-start | bytes 1572872 | tf_op jit(solution)/shard_map/ppermute | solution.py:230
  54.2 33.9 %collective-permute-start = (bf16[4096,128]{1,0:T(8,128)(2,1)S(1)}, bf16[4096,128]{1,0:T(8,128)(2,1)}, u32[]{:S(2)}, u32[]{:S(2)}) collective-permute-start(bf16[4096,128]{1,0:T(8,128)(2,1)S(1)} %bitcast.16), channel_id=1, source_target_pairs={{0,1},{1,0},{2,3},{3,2},{4,5},{5,4},{6,7},{7,6},{8,9},{9,8},{10,11... | collective-permute-start | bytes 3145736 | tf_op jit(solution)/shard_map/ppermute | solution.py:239
  56.1 18.8 %collective-permute-start.1 = (bf16[512,512]{1,0:T(8,128)(2,1)}, bf16[512,512]{1,0:T(8,128)(2,1)}, u32[]{:S(2)}, u32[]{:S(2)}) collective-permute-start(bf16[512,512]{1,0:T(8,128)(2,1)} %get-tuple-element.13), channel_id=1, source_target_pairs={{0,1},{1,0},{2,3},{3,2},{4,5},{5,4},{6,7},{7,6},{8,9},{9,8},{10,11... | collective-permute-start | bytes 1572872 | tf_op jit(solution)/shard_map/ppermute | solution.py:235
  58.5 17.2 %collective-permute-start.3 = (bf16[512,512]{1,0:T(8,128)(2,1)S(1)}, bf16[512,512]{1,0:T(8,128)(2,1)}, u32[]{:S(2)}, u32[]{:S(2)}) collective-permute-start(bf16[512,512]{1,0:T(8,128)(2,1)S(1)} %get-tuple-element.14.refs_0_), channel_id=1, source_target_pairs={{0,6},{2,0},{4,2},{6,4},{1,7},{3,1},{5,3},{7,5},{8,14},{10,8},{12,... | collective-permute-start | bytes 1572872 | tf_op jit(solution)/shard_map/ppermute | solution.py:231
  63.5 22.6 %collective-permute-start.7 = (bf16[512,512]{1,0:T(8,128)(2,1)S(1)}, bf16[512,512]{1,0:T(8,128)(2,1)}, u32[]{:S(2)}, u32[]{:S(2)}) collective-permute-start(bf16[512,512]{1,0:T(8,128)(2,1)S(1)} %collective-permute-done.5.refs_5_), channel_id=1, source_target_pairs={{0,6},{2,0},{4,2},{6,4},{1,7},{3,1},{5,3},{7,5},{8,14},{10,8},{12,... | collective-permute-start | bytes 1572872 | tf_op jit(solution)/shard_map/ppermute | solution.py:234
  72.8 15.2 %collective-permute-start.6 = (bf16[512,512]{1,0:T(8,128)(2,1)S(1)}, bf16[512,512]{1,0:T(8,128)(2,1)}, u32[]{:S(2)}, u32[]{:S(2)}) collective-permute-start(bf16[512,512]{1,0:T(8,128)(2,1)S(1)} %collective-permute-done.2.refs_2_), channel_id=1, source_target_pairs={{0,2},{2,4},{4,6},{6,0},{1,3},{3,5},{5,7},{7,1},{8,10},{10,12},{12... | collective-permute-start | bytes 1572872 | tf_op jit(solution)/shard_map/ppermute | solution.py:233
  74.9 26.2 %copy-start = (bf16[256,1024]{1,0:T(8,128)(2,1)S(1)}, bf16[256,1024]{1,0:T(8,128)(2,1)}, u32[]{:S(2)}) copy-start(bf16[256,1024]{1,0:T(8,128)(2,1)} %stored.1) | copy-start | bytes 1572868
  91.9 9.5 %copy-start.2 = (f32[256,512]{1,0:T(8,128)}, f32[256,512]{1,0:T(8,128)S(1)}, u32[]{:S(2)}) copy-start(f32[256,512]{1,0:T(8,128)S(1)} %get-tuple-element.9) | copy-start | bytes 1572868
  91.9 9.5 %copy-start.5 = (s32[384]{0:T(512)S(1)}, s32[384]{0:T(512)}, u32[]{:S(2)}) copy-start(s32[384]{0:T(512)} %param.12) | copy-start | bytes 4612
  91.9 9.5 %copy-start.6 = (s32[384]{0:T(512)S(1)}, s32[384]{0:T(512)}, u32[]{:S(2)}) copy-start(s32[384]{0:T(512)} %param.13) | copy-start | bytes 4612
  91.9 21.4 %copy-start.7 = (f32[384]{0:T(512)S(1)}, f32[384]{0:T(512)}, u32[]{:S(2)}) copy-start(f32[384]{0:T(512)} %param.15) | copy-start | bytes 4612
  92.0 34.5 %copy-start.1 = (bf16[256,1024]{1,0:T(8,128)(2,1)S(1)}, bf16[256,1024]{1,0:T(8,128)(2,1)}, u32[]{:S(2)}) copy-start(bf16[256,1024]{1,0:T(8,128)(2,1)} %stored.1) | copy-start | bytes 1572868
  101.8 29.7 %copy-start.3 = (f32[256,512]{1,0:T(8,128)S(1)}, f32[256,512]{1,0:T(8,128)}, u32[]{:S(2)}) copy-start(f32[256,512]{1,0:T(8,128)} %copy-done.2) | copy-start | bytes 1572868
  102.5 24.0 %all-to-all-start.3 = ((bf16[64,4,128]{2,1,0:T(4,128)(2,1)}), bf16[64,4,128]{2,1,0:T(4,128)(2,1)S(1)}, u32[]{:S(2)}, u32[]{:S(2)}) async-start(bf16[64,4,128]{2,1,0:T(4,128)(2,1)} %broadcast_in_dim.41), calls=%async_computation.3 | async-start | bytes 131072 | tf_op jit(solution)/shard_map/all_to_all | solution.py:31
  128.1 9.8 %all-to-all-start.4 = ((bf16[8,16,640]{2,1,0:T(8,128)(2,1)}), bf16[8,16,640]{2,1,0:T(8,128)(2,1)S(1)}, u32[]{:S(2)}, u32[]{:S(2)}) async-start(bf16[8,16,640]{2,1,0:T(8,128)(2,1)} %query_terms.1), calls=%async_computation.4 | async-start | bytes 327680 | tf_op jit(solution)/shard_map/all_to_all | solution.py:285
  141.4 4.6 %collective-permute-start.8 = (bf16[4096,128]{1,0:T(8,128)(2,1)S(1)}, bf16[4096,128]{1,0:T(8,128)(2,1)S(1)}, u32[]{:S(2)}, u32[]{:S(2)}) collective-permute-start(bf16[4096,128]{1,0:T(8,128)(2,1)S(1)} %get-tuple-element.11), channel_id=1, source_target_pairs={{0,1},{1,0},{2,3},{3,2},{4,5},{5,4},{6,7},{7,6},{8,9},{9,8},{10,11... | collective-permute-start | bytes 3145736 | tf_op jit(solution)/shard_map/ppermute | solution.py:289
  165.2 22.8 %all-to-all-start.6 = ((bf16[16,64,128]{2,1,0:T(8,128)(2,1)}), bf16[16,64,128]{2,1,0:T(8,128)(2,1)S(1)}, u32[]{:S(2)}, u32[]{:S(2)}) async-start(bf16[16,64,128]{2,1,0:T(8,128)(2,1)} %bitcast.10), calls=%async_computation.6 | async-start | bytes 524288 | tf_op jit(solution)/shard_map/all_to_all | solution.py:294
